TPU v7x, 32 devices: a whole 2x2x4 slice. The times are simulated.
32 devices in a mesh: dp: 4 (over z), expert: 8 (over y, x, core).
Axes of the slice: x: 2, y: 2, z: 4, core: 2. Of those that a mesh axis runs over, the one named last changes fastest.
Arguments:
- block_input: bfloat16 [12608, 768], P(('dp', 'expert')), may hold values from -6 to 6
- out_grad: bfloat16 [12608, 768], P(('dp', 'expert')), may hold values from -6 to 6
- expert_ids: int32 [12608, 2], P(('dp', 'expert')), may hold values from 0 to 7, all different within a row
- slot_order: int32 [32, 394], P(('dp', 'expert')), may hold values from 0 to 393, each once within a row
- joint_weight: bfloat16 [768, 2304], P('expert'), may hold values from -0.21875 to 0.21875
- out_weight: bfloat16 [768, 768], P('expert'), may hold values from -0.625 to 0.625
- router_weight: bfloat16 [768, 8], P('expert'), may hold values from -0.4375 to 0.4375
- norm_gains: bfloat16 [2, 768], P(None, 'expert'), may hold values from 0.099609375 to 1.8984375
- norm_shifts: bfloat16 [2, 768], P(None, 'expert'), may hold values from -3 to 3
- attention_bias: bfloat16 [3, 768], P(None, 'expert'), may hold values from -3 to 3
- up_weight: bfloat16 [8, 768, 3072], P('expert'), may hold values from -0.21875 to 0.21875
- down_weight: bfloat16 [8, 3072, 768], P('expert'), may hold values from -3.5 to 3.5
- up_bias: bfloat16 [8, 3072], P('expert'), may hold values from -3 to 3
- down_bias: bfloat16 [8, 768], P('expert'), may hold values from -4 to 4
Outputs:
- block_output: bfloat16 [12608, 768], P(('dp', 'expert'))
- input_grad: bfloat16 [12608, 768], P(('dp', 'expert'))
- joint_grad: float32 [768, 2304], P('expert')
- out_weight_grad: float32 [768, 768], P('expert')
- router_grad: float32 [768, 8], P('expert')
- gains_grad: float32 [2, 768], P(None, 'expert')
- shifts_grad: float32 [2, 768], P(None, 'expert')
- attention_bias_grad: float32 [3, 768], P(None, 'expert')
- up_grad: float32 [8, 768, 3072], P('expert', None, 'dp')
- down_grad: float32 [8, 3072, 768], P('expert', 'dp')
- up_bias_grad: float32 [8, 3072], P('expert', 'dp')
- down_bias_grad: float32 [8, 768], P('expert', 'dp')
Inputs may be any that keep to these rules, and one draw needn't show every extreme that they name: `expert_ids`: the two experts of a token differ. `slot_order`: each row is a permutation of the 394 token positions of one device.
All inputs are finite; a program needn't handle non-finite values.
Results may differ from a plain program's by a relative error of at most 0.024.
Values may be sent and summed in bfloat16 or wider, within the bound.
No kernel may reach another device: no remote copies, remote signals or barrier semaphores. Data moves between devices by JAX's collectives and lax.ppermute only.
A program may use at most 192 MiB of HBM per device.

v0:
```python
import functools

import jax
import jax.numpy as jnp
from jax import lax
from jax.experimental import pallas as pl
from jax.experimental.pallas import tpu as pltpu
from jax.sharding import PartitionSpec as P


HEADS = 12
HEAD_DIM = 64
SEQ = 197
LANES = 128
norm_eps = 1e-06


f32 = jnp.float32
bf16 = jnp.bfloat16
NN = ((1,), (0,))
NT = ((1,), (1,))
TN = ((0,), (0,))


def round_up(value, step):
    return (value + step - 1) // step * step


def dot(left, right, dims):
    return lax.dot_general(left, right, (dims, ((), ())), preferred_element_type=f32)


def swap(value, axis, size, offset):
    return lax.ppermute(value, axis, [(i, i ^ offset) for i in range(size)])


def exchange(chunks, axis, size):
    return [chunks[0]] + [swap(chunks[d], axis, size, d) for d in range(1, size)]


def gather_pieces(shard, axis, size):
    rows = shard.shape[0]
    if rows % 16:
        return [lax.all_gather(shard, axis, axis=0, tiled=True)], jnp.zeros((1,), jnp.int32)
    same = [shard] + [swap(shard, axis, size, d) for d in range(2, size, 2)]
    other = [swap(part, axis, size, 1) for part in same]
    pieces = [(same, other)[d % 2][d // 2] for d in range(size)]
    offsets = (lax.axis_index(axis) ^ jnp.arange(size, dtype=jnp.int32)) * rows
    return pieces, offsets


def normalise(values):
    row_mean = jnp.mean(values, axis=-1, keepdims=True)
    centered = values - row_mean
    row_var = jnp.mean(centered * centered, axis=-1, keepdims=True)
    scale = lax.rsqrt(row_var + norm_eps)
    return centered * scale, scale


def normalise_back(grads, hat, scale, gain):
    u = grads * gain
    return scale * (
        u
        - jnp.mean(u, axis=-1, keepdims=True)
        - hat * jnp.mean(u * hat, axis=-1, keepdims=True)
    )


def slot_index(ids, order, experts, capacity, stride, index):
    tokens = ids.shape[0]
    place = jnp.arange(tokens, dtype=jnp.int32)
    hits = order[:, None] == place[None, :]
    position = jnp.sum(jnp.where(hits, place[:, None], 0), axis=0)
    position_row = jnp.sum(jnp.where(hits.T, place[None, :], 0), axis=1)
    earlier = (position_row[None, :] < position[:, None]).astype(bf16)
    expert_iota = jnp.arange(experts, dtype=jnp.int32)
    hot = [(ids[:, k : k + 1] == expert_iota[None, :]) for k in range(2)]
    counts = dot(
        earlier, jnp.concatenate(hot, axis=1).astype(bf16), ((1,), (0,))
    )
    base = jnp.sum(hot[0].astype(f32), axis=0, keepdims=True)
    first = jnp.sum(jnp.where(hot[0], counts[:, :experts], 0.0), axis=1)
    second = jnp.sum(jnp.where(hot[1], counts[:, experts:] + base, 0.0), axis=1)
    rank = jnp.stack([first, second], axis=1).astype(jnp.int32)
    return jnp.where(rank < capacity, (ids ^ index) * stride + rank, experts * stride)


def shaped(shape, dtype):
    return jax.ShapeDtypeStruct(shape, dtype)


def full(shape):
    return pl.BlockSpec(shape, lambda *_: (0,) * len(shape))


def place(pieces, offsets_ref, out_ref):
    rows = pieces[0].shape[0]
    for k, piece in enumerate(pieces):
        out_ref[pl.ds(pl.multiple_of(offsets_ref[k], 16), rows), :] = piece[...]


def attend_kernel(experts, padded, offsets_ref, x_ref, *refs):
    pieces = refs[:-6]
    w_ref, par_ref, norm_ref, proj_ref, prob_ref, att_ref = refs[-6:]
    features = x_ref.shape[1]

    @pl.when(pl.program_id(0) == 0)
    def _():
        place(pieces, offsets_ref, w_ref)
        par = jnp.transpose(w_ref[:, 3 * features :].astype(f32))
        par_ref[...] = par[experts : experts + 8]

    hat, _ = normalise(x_ref[...].astype(f32))
    norm_ref[...] = (hat * par_ref[0:1] + par_ref[2:3]).astype(bf16)
    zero = jnp.zeros((1, features), f32)
    for third, bias in enumerate((par_ref[4:5], zero, par_ref[5:6])):
        cols = slice(third * features, (third + 1) * features)
        proj_ref[:, cols] = (dot(norm_ref[...], w_ref[:, cols], NN) + bias).astype(bf16)
    low = lax.broadcasted_iota(jnp.int32, (1, LANES), 1) < HEAD_DIM
    valid = lax.broadcasted_iota(jnp.int32, (1, padded), 1) < SEQ

    def pair(p, carry):
        def cols(third):
            return pl.ds(pl.multiple_of(third * features + p * LANES, LANES), LANES)

        query, key, value = (proj_ref[:, cols(third)] for third in range(3))
        outs = []
        for half in range(2):
            mine = low if half == 0 else ~low
            scores = dot(jnp.where(mine, query, jnp.zeros_like(query)), key, NT)
            scores = jnp.where(valid, scores * HEAD_DIM**-0.5, -1e30)
            powers = jnp.exp(scores - jnp.max(scores, axis=1, keepdims=True))
            probs = (powers / jnp.sum(powers, axis=1, keepdims=True)).astype(bf16)
            prob_ref[2 * p + half] = probs
            outs.append(dot(probs, value, NN))
        att_ref[:, cols(0)] = jnp.where(low, outs[0], outs[1]).astype(bf16)
        return carry

    lax.fori_loop(0, features // LANES, pair, 0, unroll=3)


def attend(x, pieces, offsets, experts, images):
    tokens, features = x.shape
    padded = tokens // images
    width = pieces[0].shape[1]
    image = lambda i, o: (i, 0)
    return pl.pallas_call(
        functools.partial(attend_kernel, experts, padded),
        grid_spec=pltpu.PrefetchScalarGridSpec(
            num_scalar_prefetch=1,
            grid=(images,),
            in_specs=[pl.BlockSpec((padded, features), image)]
            + [full(piece.shape) for piece in pieces],
            out_specs=[
                full((features, width)),
                full((8, features)),
                pl.BlockSpec((padded, features), image),
                pl.BlockSpec((padded, 3 * features), image),
                pl.BlockSpec((HEADS, padded, padded), lambda i, o: (i, 0, 0)),
                pl.BlockSpec((padded, features), image),
            ],
        ),
        out_shape=[
            shaped((features, width), bf16),
            shaped((8, features), f32),
            shaped((tokens, features), bf16),
            shaped((tokens, 3 * features), bf16),
            shaped((images * HEADS, padded, padded), bf16),
            shaped((tokens, features), bf16),
        ],
        cost_estimate=pl.CostEstimate(
            flops=12 * tokens * features * features, bytes_accessed=16 << 20, transcendentals=0
        ),
        name="attend",
    )(offsets, x, *pieces)


def hits_of(flat_ref, chunk, stride, k, width):
    lane = lax.broadcasted_iota(jnp.int32, (1, width), 1)
    wanted = jnp.where(lane < stride, lane + chunk * stride, -1)
    return flat_ref[:, k : k + 1] == wanted


def scatter_kernel(stride, flat_ref, rows_ref, *outs):
    for chunk, out in enumerate(outs):
        both = hits_of(flat_ref, chunk, stride, 0, stride) | hits_of(flat_ref, chunk, stride, 1, stride)
        out[...] = dot(both.astype(f32).astype(bf16), rows_ref[...], TN).astype(bf16)


def scatter_rows(flat, rows, experts, stride):
    features = rows.shape[1]
    return pl.pallas_call(
        functools.partial(scatter_kernel, stride),
        out_shape=[shaped((stride, features), bf16)] * experts,
        name="scatter_rows",
    )(flat, rows)


def gates_of(logits, experts):
    lane = lax.broadcasted_iota(jnp.int32, logits.shape, 1)
    logits = jnp.where(lane < experts, logits, -1e30)
    powers = jnp.exp(logits - jnp.max(logits, axis=1, keepdims=True))
    return powers / jnp.sum(powers, axis=1, keepdims=True)


def choice_of(ids_ref, k):
    lane = lax.broadcasted_iota(jnp.int32, (1, LANES), 1)
    return ids_ref[:, k : k + 1] == lane


def middle_kernel(experts, stride, capacity, offsets_ref, *refs):
    inputs = 6
    att_ref, x_ref, router_ref, par_ref, flat_ref, ids_ref = refs[:inputs]
    outs = refs[len(refs) - 4 - experts :]
    pieces = refs[inputs : len(refs) - 4 - experts]
    w_ref, residual_ref, two_ref, gate_ref = outs[:4]
    chunks = outs[4:]
    place(pieces, offsets_ref, w_ref)
    residual = x_ref[...].astype(f32) + dot(att_ref[...], w_ref[...], NN) + par_ref[6:7]
    residual_ref[...] = residual
    hat, _ = normalise(residual)
    two_ref[...] = (hat * par_ref[1:2] + par_ref[3:4]).astype(bf16)
    gates = gates_of(dot(two_ref[...], router_ref[...], NN), experts)
    gate_ref[...] = gates
    chosen = [
        jnp.sum(jnp.where(choice_of(ids_ref, k), gates, 0.0), axis=1, keepdims=True)
        for k in range(2)
    ]
    features = x_ref.shape[1]
    row = lax.broadcasted_iota(jnp.int32, (stride, 1), 0)
    blank = jnp.zeros((1, features - 3 * LANES), f32)
    for chunk, out in enumerate(chunks):
        wide = [hits_of(flat_ref, chunk, stride, k, LANES) for k in range(2)]
        slot_gate = jnp.sum(
            jnp.where(wide[0], chosen[0], 0.0) + jnp.where(wide[1], chosen[1], 0.0),
            axis=0,
            keepdims=True,
        )
        high = slot_gate.astype(bf16).astype(f32)
        rest = slot_gate - high
        middle = rest.astype(bf16).astype(f32)
        gate_row = jnp.concatenate([high, middle, rest - middle, blank], axis=1)
        both = hits_of(flat_ref, chunk, stride, 0, stride) | hits_of(flat_ref, chunk, stride, 1, stride)
        moved = dot(both.astype(f32).astype(bf16), two_ref[...], TN)
        out[...] = jnp.where(row == capacity, gate_row, moved).astype(bf16)


def middle(att, x, first_full, par, flat, ids, pieces, offsets, experts, stride, capacity):
    tokens, features = x.shape
    column = first_full.shape[1] // LANES - 1
    return pl.pallas_call(
        functools.partial(middle_kernel, experts, stride, capacity),
        grid_spec=pltpu.PrefetchScalarGridSpec(
            num_scalar_prefetch=1,
            grid=(1,),
            in_specs=[
                full(att.shape),
                full(x.shape),
                pl.BlockSpec((features, LANES), lambda i, o: (0, column)),
                full(par.shape),
                full(flat.shape),
                full(ids.shape),
            ]
            + [full(piece.shape) for piece in pieces],
            out_specs=[
                full((features, features)),
                full((tokens, features)),
                full((tokens, features)),
                full((tokens, LANES)),
            ]
            + [full((stride, features))] * experts,
        ),
        out_shape=[
            shaped((features, features), bf16),
            shaped((tokens, features), f32),
            shaped((tokens, features), bf16),
            shaped((tokens, LANES), f32),
        ]
        + [shaped((stride, features), bf16)] * experts,
        cost_estimate=pl.CostEstimate(
            flops=8 * tokens * features * features, bytes_accessed=8 << 20, transcendentals=0
        ),
        name="middle",
    )(offsets, att, x, first_full, par, flat, ids, *pieces)


GELU_A = 0.7978845608028654
GELU_B = 0.044715


def gelu_half(v):
    return 0.5 + 0.5 * jnp.tanh(v * (GELU_A + (GELU_A * GELU_B) * (v * v)))


def gelu_slope(v):
    square = v * v
    half = 0.5 + 0.5 * jnp.tanh(v * (GELU_A + (GELU_A * GELU_B) * square))
    bend = (v * half) * (1.0 - half)
    return half + bend * (2.0 * GELU_A + (6.0 * GELU_A * GELU_B) * square)


def expert_forward_kernel(count, capacity, *refs):
    xs, gs = refs[:count], refs[count : 2 * count]
    up_ref, bias_ref, x_ref, sg_ref, hid_ref, pre_ref, grad_ref = refs[2 * count :]
    stride = xs[0].shape[0]
    slots = x_ref.shape[0]

    @pl.when(pl.program_id(0) == 0)
    def _():
        eye = lax.broadcasted_iota(jnp.int32, (stride, LANES), 0) == lax.broadcasted_iota(
            jnp.int32, (stride, LANES), 1
        )
        for d in range(count):
            rows = slice(d * stride, (d + 1) * stride)
            x_ref[rows, :] = xs[d][...]
            tail = xs[d][stride - 16 :, :].astype(f32)
            at = capacity - (stride - 16)
            parts = tail[at : at + 1]
            gate = parts[:, :LANES] + parts[:, LANES : 2 * LANES] + parts[:, 2 * LANES : 3 * LANES]
            gate = jnp.sum(jnp.where(eye, gate, 0.0), axis=1, keepdims=True)
            sg_ref[rows, :] = (gate * gs[d][...].astype(f32)).astype(bf16)

    block = 256
    for m in range(0, slots, block):
        rows = slice(m, m + block)
        v = dot(x_ref[rows, :], up_ref[...], NN) + bias_ref[...]
        hid_ref[rows, :] = (v * gelu_half(v)).astype(bf16)
        pre_ref[rows, :] = v.astype(bf16)
    for n in range(0, hid_ref.shape[1], block):
        cols = slice(n, n + block)
        grad_ref[cols, :] = dot(hid_ref[:, cols], sg_ref[...], TN).astype(bf16)


def expert_forward(xs, gs, up, up_bias, capacity, tile=768):
    count = len(xs)
    stride, features = xs[0].shape
    slots, units = count * stride, up.shape[1]
    return pl.pallas_call(
        functools.partial(expert_forward_kernel, count, capacity),
        grid=(units // tile,),
        in_specs=[full((stride, features))] * (2 * count)
        + [
            pl.BlockSpec((features, tile), lambda j: (0, j)),
            pl.BlockSpec((1, tile), lambda j: (0, j)),
        ],
        out_specs=[
            full((slots, features)),
            full((slots, features)),
            pl.BlockSpec((slots, tile), lambda j: (0, j)),
            pl.BlockSpec((slots, tile), lambda j: (0, j)),
            pl.BlockSpec((tile, features), lambda j: (j, 0)),
        ],
        out_shape=[
            shaped((slots, features), bf16),
            shaped((slots, features), bf16),
            shaped((slots, units), bf16),
            shaped((slots, units), bf16),
            shaped((units, features), bf16),
        ],
        cost_estimate=pl.CostEstimate(
            flops=4 * slots * features * units, bytes_accessed=30 << 20, transcendentals=0
        ),
        name="expert_forward",
    )(*xs, *gs, up, up_bias)


def accumulate(acc_ref, value, initial=None):
    @pl.when(pl.program_id(0) == 0)
    def _():
        acc_ref[...] = value if initial is None else value + initial

    @pl.when(pl.program_id(0) > 0)
    def _():
        acc_ref[...] += value


def emit_chunks(acc_ref, outs):
    @pl.when(pl.program_id(0) == pl.num_programs(0) - 1)
    def _():
        stride = acc_ref.shape[0] // len(outs)
        for d, out in enumerate(outs):
            out[...] = acc_ref[d * stride : (d + 1) * stride, :].astype(bf16)


def expert_out_kernel(count, hid_ref, down_ref, bias_ref, *refs):
    outs, acc_ref = refs[:count], refs[count]
    accumulate(acc_ref, dot(hid_ref[...], down_ref[...], NN), bias_ref[...])
    emit_chunks(acc_ref, outs)


def expert_out(hidden, down, bias, count, tile=768):
    slots, units = hidden.shape
    features = down.shape[1]
    return pl.pallas_call(
        functools.partial(expert_out_kernel, count),
        grid=(units // tile,),
        in_specs=[
            pl.BlockSpec((slots, tile), lambda j: (0, j)),
            pl.BlockSpec((tile, features), lambda j: (j, 0)),
            full((1, features)),
        ],
        out_specs=[full((slots // count, features))] * count,
        out_shape=[shaped((slots // count, features), bf16)] * count,
        scratch_shapes=[pltpu.VMEM((slots, features), f32)],
        cost_estimate=pl.CostEstimate(
            flops=2 * slots * features * units, bytes_accessed=12 << 20, transcendentals=0
        ),
        name="expert_out",
    )(hidden, down, bias)


def expert_back_kernel(count, sg_ref, down_ref, pre_ref, up_ref, inner_ref, sums_ref, *refs):
    outs, acc_ref = refs[:count], refs[count]
    slots, block = acc_ref.shape[0], 256
    total = jnp.zeros(sums_ref.shape, f32)
    for m in range(0, slots, block):
        rows = slice(m, m + block)
        slope = gelu_slope(pre_ref[rows, :].astype(f32))
        low = (dot(sg_ref[rows, :], down_ref[...], NT) * slope).astype(bf16)
        inner_ref[rows, :] = low
        total += jnp.sum(low.astype(f32), axis=0, keepdims=True)
    sums_ref[...] = total
    accumulate(acc_ref, dot(inner_ref[...], up_ref[...], NT))
    emit_chunks(acc_ref, outs)


def expert_back(slot_grad, down, pre, up, count, tile=768):
    slots, features = slot_grad.shape
    units = up.shape[1]
    return pl.pallas_call(
        functools.partial(expert_back_kernel, count),
        grid=(units // tile,),
        in_specs=[
            full((slots, features)),
            pl.BlockSpec((tile, features), lambda j: (j, 0)),
            pl.BlockSpec((slots, tile), lambda j: (0, j)),
            pl.BlockSpec((features, tile), lambda j: (0, j)),
        ],
        out_specs=[
            pl.BlockSpec((slots, tile), lambda j: (0, j)),
            pl.BlockSpec((1, tile), lambda j: (0, j)),
        ]
        + [full((slots // count, features))] * count,
        out_shape=[shaped((slots, units), bf16), shaped((1, units), f32)]
        + [shaped((slots // count, features), bf16)] * count,
        scratch_shapes=[pltpu.VMEM((slots, features), f32)],
        cost_estimate=pl.CostEstimate(
            flops=4 * slots * features * units, bytes_accessed=24 << 20, transcendentals=0
        ),
        name="expert_back",
    )(slot_grad, down, pre, up)


def up_gradient_kernel(x_ref, inner_ref, out_ref):
    block = 256
    for n in range(0, x_ref.shape[1], block):
        cols = slice(n, n + block)
        out_ref[cols, :] = dot(x_ref[:, cols], inner_ref[...], TN).astype(bf16)


def up_gradient(x, inner, tile=768):
    slots, features = x.shape
    units = inner.shape[1]
    return pl.pallas_call(
        up_gradient_kernel,
        grid=(units // tile,),
        in_specs=[full((slots, features)), pl.BlockSpec((slots, tile), lambda j: (0, j))],
        out_specs=pl.BlockSpec((features, tile), lambda j: (0, j)),
        out_shape=shaped((features, units), bf16),
        cost_estimate=pl.CostEstimate(
            flops=2 * slots * features * units, bytes_accessed=12 << 20, transcendentals=0
        ),
        name="up_gradient",
    )(x, inner)


def combine_kernel(experts, stride, *refs):
    chunks = refs[:experts]
    flat_ref, ids_ref, gate_ref, residual_ref, grad_ref, out_ref, logit_ref = refs[experts:-1]
    rows_ref = refs[-1]
    for d in range(experts):
        rows_ref[d * stride : (d + 1) * stride, :] = chunks[d][...]
    slots = experts * stride
    slot = lax.broadcasted_iota(jnp.int32, (1, slots), 1)
    gates = gate_ref[...]
    grads = grad_ref[...].astype(f32)
    total = residual_ref[...]
    mass = jnp.zeros_like(gates)
    for k in range(2):
        hits = (flat_ref[:, k : k + 1] == slot).astype(f32).astype(bf16)
        picked = dot(hits, rows_ref[...], NN)
        choice = choice_of(ids_ref, k)
        total += jnp.sum(jnp.where(choice, gates, 0.0), axis=1, keepdims=True) * picked
        gate_grad = jnp.sum(grads * picked, axis=1, keepdims=True)
        mass += jnp.where(choice, gate_grad, 0.0)
    out_ref[...] = total.astype(bf16)
    logit_ref[...] = (gates * (mass - jnp.sum(gates * mass, axis=1, keepdims=True))).astype(bf16)


def combine(chunks, flat, ids, gates, residual, grad_low):
    experts, (stride, features) = len(chunks), chunks[0].shape
    tokens = residual.shape[0]
    return pl.pallas_call(
        functools.partial(combine_kernel, experts, stride),
        out_shape=[shaped((tokens, features), bf16), shaped((tokens, LANES), bf16)],
        scratch_shapes=[pltpu.VMEM((experts * stride, features), bf16)],
        cost_estimate=pl.CostEstimate(
            flops=4 * tokens * experts * stride * features, bytes_accessed=6 << 20, transcendentals=0
        ),
        name="combine",
    )(*chunks, flat, ids, gates, residual, grad_low)


def split_rows(value_ref, offsets_ref, width, kept_ref, sent_ref):
    blocks = 2 * kept_ref.shape[0]
    rows = kept_ref.shape[1]
    for d in range(blocks):
        part = value_ref[pl.ds(pl.multiple_of(offsets_ref[d], 8), rows), :].astype(bf16)
        (kept_ref, sent_ref)[d % 2][d // 2, :, width] = part


def residual_back_kernel(experts, stride, offsets_ref, *refs):
    chunks = refs[:experts]
    (
        flat_ref,
        logit_ref,
        router_ref,
        two_ref,
        residual_ref,
        grad_ref,
        par_ref,
        w_ref,
        att_ref,
        residual_grad_ref,
        att_grad_ref,
        kept_ref,
        sent_ref,
        rows_ref,
        vector_ref,
        value_ref,
        small_ref,
    ) = refs[experts:]
    for d in range(experts):
        rows_ref[d * stride : (d + 1) * stride, :] = chunks[d][...]
    features = residual_ref.shape[1]
    slot = lax.broadcasted_iota(jnp.int32, (1, experts * stride), 1)
    hits = (flat_ref[:, 0:1] == slot) | (flat_ref[:, 1:2] == slot)
    two_grad = dot(hits.astype(f32).astype(bf16), rows_ref[...], NN)
    two_grad += dot(logit_ref[...], router_ref[...], NT)
    hat, scale = normalise(residual_ref[...])
    residual_grad = grad_ref[...].astype(f32) + normalise_back(two_grad, hat, scale, par_ref[1:2])
    residual_grad_ref[...] = residual_grad
    branch = residual_grad.astype(bf16)
    vector_ref[...] = jnp.zeros_like(vector_ref)
    vector_ref[0:1] = jnp.sum(two_grad * hat, axis=0, keepdims=True)
    vector_ref[1:2] = jnp.sum(two_grad, axis=0, keepdims=True)
    vector_ref[2:3] = jnp.sum(residual_grad, axis=0, keepdims=True)
    att_grad_ref[...] = dot(branch, w_ref[...], NT).astype(bf16)
    value_ref[...] = dot(att_ref[...], branch, TN)
    split_rows(value_ref, offsets_ref, slice(0, features), kept_ref, sent_ref)
    small_ref[...] = dot(two_ref[...], logit_ref[...], TN)
    split_rows(small_ref, offsets_ref, slice(features, features + LANES), kept_ref, sent_ref)
    small_ref[...] = jnp.transpose(vector_ref[...])
    split_rows(
        small_ref, offsets_ref, slice(features + LANES, features + 2 * LANES), kept_ref, sent_ref
    )


def residual_back(
    chunks, flat, logit_grad, first_full, two, residual, grad_low, par, w, att, offsets
):
    experts, (stride, features) = len(chunks), chunks[0].shape
    tokens = residual.shape[0]
    column = first_full.shape[1] // LANES - 1
    size = offsets.shape[0]
    packed = (size // 2, features // size, features + 2 * LANES)
    return pl.pallas_call(
        functools.partial(residual_back_kernel, experts, stride),
        grid_spec=pltpu.PrefetchScalarGridSpec(
            num_scalar_prefetch=1,
            grid=(1,),
            in_specs=[full((stride, features))] * experts
            + [
                full(flat.shape),
                full(logit_grad.shape),
                pl.BlockSpec((features, LANES), lambda i, o: (0, column)),
            ]
            + [full(value.shape) for value in (two, residual, grad_low, par, w, att)],
            out_specs=[full((tokens, features))] * 2 + [full(packed)] * 2,
            scratch_shapes=[
                pltpu.VMEM((experts * stride, features), bf16),
                pltpu.VMEM((LANES, features), f32),
                pltpu.VMEM((features, features), f32),
                pltpu.VMEM((features, LANES), f32),
            ],
        ),
        out_shape=[
            shaped((tokens, features), f32),
            shaped((tokens, features), bf16),
            shaped(packed, bf16),
            shaped(packed, bf16),
        ],
        cost_estimate=pl.CostEstimate(
            flops=8 * tokens * features * features, bytes_accessed=10 << 20, transcendentals=0
        ),
        name="residual_back",
    )(
        offsets, *chunks, flat, logit_grad, first_full, two, residual, grad_low, par, w, att
    )


def attend_back_kernel(proj_ref, prob_ref, out_grad_ref, grad_ref):
    features = out_grad_ref.shape[1]
    low = lax.broadcasted_iota(jnp.int32, (1, LANES), 1) < HEAD_DIM

    def pair(p, carry):
        def cols(third):
            return pl.ds(pl.multiple_of(third * features + p * LANES, LANES), LANES)

        query, key, value = (proj_ref[:, cols(third)] for third in range(3))
        grads = out_grad_ref[:, cols(0)]
        results = []
        for half in range(2):
            mine = low if half == 0 else ~low
            low_probs = prob_ref[2 * p + half]
            probs = low_probs.astype(f32)
            weight_grad = dot(jnp.where(mine, grads, jnp.zeros_like(grads)), value, NT)
            total = jnp.sum(weight_grad * probs, axis=1, keepdims=True)
            score_grad = (probs * (weight_grad - total)).astype(bf16)
            results.append(
                (
                    dot(score_grad, key, NN) * HEAD_DIM**-0.5,
                    dot(score_grad, query, TN) * HEAD_DIM**-0.5,
                    dot(low_probs, grads, TN),
                )
            )
        for third in range(3):
            grad_ref[:, cols(third)] = jnp.where(
                low, results[0][third], results[1][third]
            ).astype(bf16)
        return carry

    lax.fori_loop(0, features // LANES, pair, 0, unroll=3)


def attend_back(proj, probs, out_grad, images):
    tokens, features = out_grad.shape
    padded = tokens // images
    image = lambda i: (i, 0)
    return pl.pallas_call(
        attend_back_kernel,
        grid=(images,),
        in_specs=[
            pl.BlockSpec((padded, 3 * features), image),
            pl.BlockSpec((HEADS, padded, padded), lambda i: (i, 0, 0)),
            pl.BlockSpec((padded, features), image),
        ],
        out_specs=pl.BlockSpec((padded, 3 * features), image),
        out_shape=shaped((tokens, 3 * features), bf16),
        cost_estimate=pl.CostEstimate(
            flops=12 * tokens * features * features, bytes_accessed=6 << 20, transcendentals=0
        ),
        name="attend_back",
    )(proj, probs, out_grad)


def input_back_kernel(
    offsets_ref,
    norm_ref,
    grad_ref,
    w_ref,
    x_ref,
    residual_grad_ref,
    par_ref,
    out_ref,
    kept_ref,
    sent_ref,
    acc_ref,
    vector_ref,
    value_ref,
    small_ref,
):
    features = x_ref.shape[1]
    vector_ref[...] = jnp.zeros_like(vector_ref)
    for third in range(3):
        cols = slice(third * features, (third + 1) * features)
        value_ref[...] = dot(norm_ref[...], grad_ref[:, cols], TN)
        split_rows(value_ref, offsets_ref, cols, kept_ref, sent_ref)
        value = dot(grad_ref[:, cols], w_ref[:, cols], NT)
        if third == 0:
            acc_ref[...] = value
        else:
            acc_ref[...] += value
        if third != 1:
            row = 2 + third // 2
            vector_ref[row : row + 1] = jnp.sum(
                grad_ref[:, cols].astype(f32), axis=0, keepdims=True
            )
    hat, scale = normalise(x_ref[...].astype(f32))
    grads = acc_ref[...]
    vector_ref[0:1] = jnp.sum(grads * hat, axis=0, keepdims=True)
    vector_ref[1:2] = jnp.sum(grads, axis=0, keepdims=True)
    small_ref[...] = jnp.transpose(vector_ref[...])
    split_rows(
        small_ref, offsets_ref, slice(3 * features, 3 * features + LANES), kept_ref, sent_ref
    )
    out_ref[...] = (
        residual_grad_ref[...] + normalise_back(grads, hat, scale, par_ref[0:1])
    ).astype(bf16)


def input_back(norm, grads, first_full, x, residual_grad, par, offsets):
    tokens, features = x.shape
    size = offsets.shape[0]
    packed = (size // 2, features // size, 3 * features + LANES)
    return pl.pallas_call(
        input_back_kernel,
        grid_spec=pltpu.PrefetchScalarGridSpec(
            num_scalar_prefetch=1,
            grid=(1,),
            in_specs=[full(norm.shape), full(grads.shape), full((features, 3 * features))]
            + [full(value.shape) for value in (x, residual_grad, par)],
            out_specs=[full((tokens, features))] + [full(packed)] * 2,
            scratch_shapes=[
                pltpu.VMEM((tokens, features), f32),
                pltpu.VMEM((LANES, features), f32),
                pltpu.VMEM((features, features), f32),
                pltpu.VMEM((features, LANES), f32),
            ],
        ),
        out_shape=[shaped((tokens, features), bf16), shaped(packed, bf16), shaped(packed, bf16)],
        cost_estimate=pl.CostEstimate(
            flops=12 * tokens * features * features, bytes_accessed=16 << 20, transcendentals=0
        ),
        name="input_back",
    )(offsets, norm, grads, first_full, x, residual_grad, par)


def reduce_blocks(kept, sent, expert_size, dp_size, dp_index):
    pair_sum = (
        kept.astype(f32) + swap(sent, "expert", expert_size, 1).astype(f32)
    ).astype(bf16)
    parts = [pair_sum[0]] + [
        swap(pair_sum[d // 2], "expert", expert_size, d) for d in range(2, expert_size, 2)
    ]
    plane_sum = sum(part.astype(f32) for part in parts).astype(bf16)
    plane_sum = plane_sum.reshape(dp_size, plane_sum.shape[0] // dp_size, -1)
    dp_parts = exchange(
        [
            lax.dynamic_index_in_dim(plane_sum, dp_index ^ d, 0, keepdims=False)
            for d in range(dp_size)
        ],
        "dp",
        dp_size,
    )
    dp_sum = sum(part.astype(f32) for part in dp_parts).astype(bf16)
    return lax.all_gather(dp_sum, "dp", axis=0, tiled=True).astype(f32)


def per_device(
    block_input,
    out_grad,
    expert_ids,
    slot_order,
    joint_weight,
    out_weight,
    router_weight,
    norm_gains,
    norm_shifts,
    attention_bias,
    up_weight,
    down_weight,
    up_bias,
    down_bias,
    *,
    expert_size,
    dp_size,
):
    index = lax.axis_index("expert")
    dp_index = lax.axis_index("dp")
    row_count, features = block_input.shape
    images = row_count // SEQ
    experts = router_weight.shape[1]
    capacity = max(2, (5 * row_count + 2 * experts - 1) // (2 * experts))
    stride = round_up(capacity + 1, 16)
    slots = experts * stride
    padded = round_up(SEQ, 16)
    tokens = images * padded
    hidden_units = up_weight.shape[2]
    block_rows = features // expert_size
    row_offsets = (index ^ jnp.arange(expert_size, dtype=jnp.int32)) * block_rows

    def pad_rows(values, fill=0):
        split = values.reshape(images, SEQ, values.shape[-1])
        return jnp.pad(
            split, ((0, 0), (0, padded - SEQ), (0, 0)), constant_values=fill
        ).reshape(tokens, values.shape[-1])

    def crop_rows(values):
        return values.reshape(images, padded, -1)[:, :SEQ].reshape(row_count, -1)

    small = jnp.concatenate(
        [router_weight, norm_gains.T, norm_shifts.T, attention_bias.T], axis=1
    )
    small = jnp.pad(small, ((0, 0), (0, LANES - small.shape[1])))
    first, first_offsets = gather_pieces(
        jnp.concatenate([joint_weight, small], axis=1), "expert", expert_size
    )
    input_low, grad_low = pad_rows(block_input), pad_rows(out_grad)
    ids = pad_rows(expert_ids)
    flat = pad_rows(
        slot_index(expert_ids, slot_order[0], experts, capacity, stride, index), slots
    )
    grad_slots = scatter_rows(flat, grad_low, experts, stride)
    first, grad_slots, out_shard = lax.optimization_barrier((first, grad_slots, out_weight))
    second, second_offsets = gather_pieces(out_shard, "expert", expert_size)
    grad_arrived = exchange(grad_slots, "expert", expert_size)

    first_full, par, normed, projected, probs, attended = attend(
        input_low, first, first_offsets, experts, images
    )
    out_full, residual, two_low, gates, *dispatched = middle(
        attended,
        input_low,
        first_full,
        par,
        flat,
        ids,
        second,
        second_offsets,
        experts,
        stride,
        capacity,
    )
    arrived = exchange(dispatched, "expert", expert_size)

    up, down = up_weight[0], down_weight[0]
    rows, slot_grad, hidden, pre, down_local = expert_forward(
        arrived, grad_arrived, up, up_bias.astype(f32), capacity
    )
    down_part = lax.psum_scatter(down_local, "dp", scatter_dimension=0, tiled=True)
    expert_low = expert_out(hidden, down, down_bias.astype(f32), experts)
    slot_grad, expert_low = lax.optimization_barrier((slot_grad, expert_low))
    returned = exchange(expert_low, "expert", expert_size)
    inner, inner_sums, *rows_grad = expert_back(slot_grad, down, pre, up, experts)
    rows_back = exchange(rows_grad, "expert", expert_size)
    up_local = up_gradient(rows, inner)
    up_part = lax.psum_scatter(up_local, "dp", scatter_dimension=1, tiled=True)
    bias_local = jnp.concatenate(
        [
            inner_sums.reshape(dp_size, -1),
            jnp.sum(slot_grad, axis=0, dtype=f32).reshape(dp_size, -1),
        ],
        axis=1,
    )
    bias_chunks = [
        lax.dynamic_index_in_dim(bias_local, dp_index ^ d, 0) for d in range(dp_size)
    ]
    bias_sum = sum(exchange(bias_chunks, "dp", dp_size))
    up_bias_grad = bias_sum[:, : hidden_units // dp_size]
    down_bias_grad = bias_sum[:, hidden_units // dp_size :]

    block_output, logit_grad = combine(returned, flat, ids, gates, residual, grad_low)
    residual_grad, attended_grad, kept, sent = residual_back(
        rows_back,
        flat,
        logit_grad,
        first_full,
        two_low,
        residual,
        grad_low,
        par,
        out_full,
        attended,
        row_offsets,
    )
    late = reduce_blocks(kept, sent, expert_size, dp_size, dp_index)
    projected_grad = attend_back(projected, probs, attended_grad, images)
    input_grad, kept, sent = input_back(
        normed, projected_grad, first_full, input_low, residual_grad, par, row_offsets
    )
    early = reduce_blocks(kept, sent, expert_size, dp_size, dp_index)
    late_vectors = late[:, features + LANES : features + LANES + 3].T
    early_vectors = early[:, 3 * features : 3 * features + 4].T
    return (
        crop_rows(block_output),
        crop_rows(input_grad),
        early[:, : 3 * features],
        late[:, :features],
        late[:, features : features + experts],
        jnp.stack([early_vectors[0], late_vectors[0]]),
        jnp.stack([early_vectors[1], late_vectors[1]]),
        jnp.stack([early_vectors[2], early_vectors[3], late_vectors[2]]),
        up_part[None].astype(f32),
        down_part[None].astype(f32),
        up_bias_grad,
        down_bias_grad,
    )


def solution(mesh):
    def body(*args):
        return per_device(
            *args, expert_size=mesh.shape["expert"], dp_size=mesh.shape["dp"]
        )

    in_specs = (
        P(("dp", "expert"), None),
        P(("dp", "expert"), None),
        P(("dp", "expert"), None),
        P(("dp", "expert"), None),
        P("expert", None),
        P("expert", None),
        P("expert", None),
        P(None, "expert"),
        P(None, "expert"),
        P(None, "expert"),
        P("expert", None, None),
        P("expert", None, None),
        P("expert", None),
        P("expert", None),
    )
    out_specs = (
        P(("dp", "expert"), None),
        P(("dp", "expert"), None),
        P("expert", None),
        P("expert", None),
        P("expert", None),
        P(None, "expert"),
        P(None, "expert"),
        P(None, "expert"),
        P("expert", None, "dp"),
        P("expert", "dp", None),
        P("expert", "dp"),
        P("expert", "dp"),
    )
    return jax.shard_map(
        body, mesh=mesh, in_specs=in_specs, out_specs=out_specs, check_vma=False
    )
```

profile of v0, /device:TPU:0, one launch (start us, length us, event | category | flops | bytes accessed | tf_op | source)
XLA Modules:
  0.0 370.8 jit_solution(16953468236224666362)
XLA Ops:
  9.8 2.6 collective-permute-start.1
  15.7 8.2 %collective-permute-done.1.refs_2_ = bf16[96,2432]{1,0:T(8,128)(2,1)S(1)} collective-permute-done((bf16[96,2432]{1,0:T(8,128)(2,1)S(1)}, bf16[96,2432]{1,0:T(8,128)(2,1)S(1)}, u32[]{:S(2)}, u32[]{:S(2)}) %collective-permute-start.1) | collective-permute-done | bytes 466976 | tf_op jit(solution)/shard_map/ppermute | solution.py:34
  23.9 11.3 %collective-permute-done.3.refs_4_ = bf16[96,2432]{1,0:T(8,128)(2,1)} collective-permute-done((bf16[96,2432]{1,0:T(8,128)(2,1)S(1)}, bf16[96,2432]{1,0:T(8,128)(2,1)}, u32[]{:S(2)}, u32[]{:S(2)}) %collective-permute-start.3) | collective-permute-done | bytes 466976 | tf_op jit(solution)/shard_map/ppermute | solution.py:34
  39.0 4.0 %scatter_rows.1 = (bf16[128,768]{1,0:T(8,128)(2,1)}, bf16[128,768]{1,0:T(8,128)(2,1)}, bf16[128,768]{1,0:T(8,128)(2,1)}, bf16[128,768]{1,0:T(8,128)(2,1)}, bf16[...) custom-call(s32[416,2]{1,0:T(8,128)} %bitcast.75, ...), custom_call_target="tpu_custom_call" | custom-call | tf_op jit(solution)/shard_map/scatter_rows/pallas_call | solution.py:192
  46.6 2.7 collective-permute-done.8.refs_8_
  58.8 13.8 %attend.1 = (bf16[768,2432]{1,0:T(8,128)(2,1)}, f32[8,768]{1,0:T(8,128)}, bf16[416,768]{1,0:T(8,128)(2,1)}, bf16[416,2304]{1,0:T(8,128)(2,1)}, bf16[24,208,208]{2,1,0:T(8,128)(2,1)}, /*index=5*/bf16[416,768]{1,0:T(8,128)(2,1)}) custom-call(s32[8]{0:T(128)} %xor_multiply_fusion.offsets_ref, bf16[416,768]{1,0:T(8,128)(2,1)} %bitcast.83, ...), custom_call_target="tpu_custom_call" | custom-call | flops 2944401408 | bytes 16777216 | tf_op jit(solution)/shard_map/attend/pallas_call | solution.py:147
  73.4 7.0 %middle.1 = (bf16[768,768]{1,0:T(8,128)(2,1)}, f32[416,768]{1,0:T(8,128)}, bf16[416,768]{1,0:T(8,128)(2,1)}, f32[416,128]{1,0:T(8,128)}, bf16[128,768]{1,0:T(8,1...) custom-call(s32[8]{0:T(128)} %xor_multiply_fusion.offsets_ref, ...), custom_call_target="tpu_custom_call" | custom-call | flops 1962934272 | bytes 8388608 | tf_op jit(solution)/shard_map/middle/pallas_call | solution.py:251
  85.1 4.0 %collective-permute-done.26.refs_14_ = bf16[128,768]{1,0:T(8,128)(2,1)S(1)} collective-permute-done((bf16[128,768]{1,0:T(8,128)(2,1)S(1)}, bf16[128,768]{1,0:T(8,128)(2,1)S(1)}, u32[]{:S(2)}, u32[]{:S(2)}) %collective-permute-start.26) | collective-permute-done | bytes 196640 | tf_op jit(solution)/shard_map/ppermute | solution.py:34
  100.6 5.4 %collective-permute-done.19.refs_6_ = bf16[128,768]{1,0:T(8,128)(2,1)S(1)} collective-permute-done((bf16[128,768]{1,0:T(8,128)(2,1)}, bf16[128,768]{1,0:T(8,128)(2,1)S(1)}, u32[]{:S(2)}, u32[]{:S(2)}) %collective-permute-start.19) | collective-permute-done | bytes 196640 | tf_op jit(solution)/shard_map/ppermute | solution.py:34
  106.0 2.6 collective-permute-done.20.refs_7_
  109.3 15.3 %expert_forward.1 = (bf16[1024,768]{1,0:T(8,128)(2,1)}, bf16[1024,768]{1,0:T(8,128)(2,1)}, bf16[1024,3072]{1,0:T(8,128)(2,1)}, bf16[1024,3072]{1,0:T(8,128)(2,1)}, bf16[3072,768]{1,0:T(8,128)(2,1)}) custom-call(bf16[128,768]{1,0:T(8,128)(2,1)} %get-tuple-element.116.refs_0_, bf16[128,768]{1,0:T(8,128)(2,1)} %copy-done.43, bf16[128,768]{1,0:T(8,128)(2,1)} %copy-done.47, ...), custom_call_target="tpu_custom_call" | custom-call | flops 9663676416 | bytes 31457280 | tf_op jit(solution)/shard_map/expert_forward/pallas_call | solution.py:338
  124.6 9.9 %expert_out.1 = (bf16[128,768]{1,0:T(8,128)(2,1)}, bf16[128,768]{1,0:T(8,128)(2,1)}, bf16[128,768]{1,0:T(8,128)(2,1)}, bf16[128,768]{1,0:T(8,128)(2,1)}, bf16[12...) custom-call(bf16[1024,3072]{1,0:T(8,128)(2,1)} %get-tuple-element.133.hid_ref, ...), custom_call_target="tpu_custom_call" | custom-call | flops 4831838208 | bytes 12582912 | tf_op jit(solution)/shard_map/expert_out/pallas_call | solution.py:394
  134.5 20.6 %expert_back.1 = (bf16[1024,3072]{1,0:T(8,128)(2,1)}, f32[1,3072]{1,0:T(1,128)}, bf16[128,768]{1,0:T(8,128)(2,1)}, bf16[128,768]{1,0:T(8,128)(2,1)}, bf16[128,76...) custom-call(bf16[1024,768]{1,0:T(8,128)(2,1)} %get-tuple-element.156, ...), custom_call_target="tpu_custom_call" | custom-call | flops 9663676416 | bytes 25165824 | tf_op jit(solution)/shard_map/expert_back/pallas_call | solution.py:430
  155.1 9.2 %up_gradient.1 = bf16[768,3072]{1,0:T(8,128)(2,1)} custom-call(bf16[1024,768]{1,0:T(8,128)(2,1)} %get-tuple-element.176.x_ref, bf16[1024,3072]{1,0:T(8,128)(2,1)} %get-tuple-element.177.inner_ref), custom_call_target="tpu_custom_call" | custom-call | flops 4831838208 | bytes 12582912 | tf_op jit(solution)/shard_map/up_gradient/pallas_call | solution.py:464
  174.4 2.7 collective-permute-done.30.refs_3_
  179.9 7.2 %collective-permute-done.32.refs_5_ = bf16[128,768]{1,0:T(8,128)(2,1)S(1)} collective-permute-done((bf16[128,768]{1,0:T(8,128)(2,1)S(1)}, bf16[128,768]{1,0:T(8,128)(2,1)S(1)}, u32[]{:S(2)}, u32[]{:S(2)}) %collective-permute-start.32) | collective-permute-done | bytes 196640 | tf_op jit(solution)/shard_map/ppermute | solution.py:34
  193.5 4.9 %combine.1 = (bf16[416,768]{1,0:T(8,128)(2,1)}, bf16[416,128]{1,0:T(8,128)(2,1)}) custom-call(bf16[128,768]{1,0:T(8,128)(2,1)} %get-tuple-element.142.refs_0_, bf16[128,768]{1,0:T(8,128)(2,1)} %copy-done.38, bf16[128,768]{1,0:T(8,128)(2,1)} %copy-done.41, bf16[128,768]{1,0:T(8,128)(2,1)} %copy-done.42, bf16[128,768]{1,0:T(8,128)(2,1)} %copy-done.45, ...), custom_call_target="tpu_custom_call" | custom-call | flops 1308622848 | bytes 6291456 | tf_op jit(solution)/shard_map/combine/pallas_call | solution.py:503
  198.4 6.6 %collective-permute-done.38.refs_4_ = bf16[128,768]{1,0:T(8,128)(2,1)S(1)} collective-permute-done((bf16[128,768]{1,0:T(8,128)(2,1)S(1)}, bf16[128,768]{1,0:T(8,128)(2,1)S(1)}, u32[]{:S(2)}, u32[]{:S(2)}) %collective-permute-start.38) | collective-permute-done | bytes 196640 | tf_op jit(solution)/shard_map/ppermute | solution.py:34
  208.1 8.1 %residual_back.1 = (f32[416,768]{1,0:T(8,128)}, bf16[416,768]{1,0:T(8,128)(2,1)}, bf16[4,96,1024]{2,1,0:T(8,128)(2,1)}, bf16[4,96,1024]{2,1,0:T(8,128)(2,1)}) custom-call(s32[8]{0:T(128)} %xor_multiply_fusion.offsets_ref, bf16[128,768]{1,0:T(8,128)(2,1)} %get-tuple-element.158.refs_0_, bf16[128,768]{1,0:T(8,128)(2,1)} %copy-done.6, ...), custom_call_target="tpu_custom_call" | custom-call | flops 1962934272 | bytes 10485760 | tf_op jit(solution)/shard_map/residual_back/pallas_call | solution.py:577
  217.4 12.2 %attend_back.1.grad_ref = bf16[416,2304]{1,0:T(8,128)(2,1)} custom-call(bf16[416,2304]{1,0:T(8,128)(2,1)} %get-tuple-element.154.proj_ref, bf16[24,208,208]{2,1,0:T(8,128)(2,1)} %get-tuple-element.155.prob_ref, bf16[416,768]{1,0:T(8,128)(2,1)} %get-tuple-element.169.out_grad_ref), custom_call_target="tpu_custom_call" | custom-call | flops 2944401408 | bytes 6291456 | tf_op jit(solution)/shard_map/attend_back/pallas_call | solution.py:650
  229.6 11.1 %input_back.1 = (bf16[416,768]{1,0:T(8,128)(2,1)}, bf16[4,96,2432]{2,1,0:T(8,128)(2,1)}, bf16[4,96,2432]{2,1,0:T(8,128)(2,1)}) custom-call(s32[8]{0:T(128)} %xor_multiply_fusion.offsets_ref, bf16[416,768]{1,0:T(8,128)(2,1)} %get-tuple-element.153.norm_ref, bf16[416,2304]{1,0:T(8,128)(2,1)} %attend_back.1.grad_ref, ...), custom_call_target="tpu_custom_call" | custom-call | flops 2944401408 | bytes 16777216 | tf_op jit(solution)/shard_map/input_back/pallas_call | solution.py:716
  242.3 3.6 collective-permute-start.58
  258.3 3.0 collective-permute-done.51
  262.6 3.5 collective-permute-start.55
  276.8 17.5 %all_gather.7 = bf16[96,1024]{1,0:T(8,128)(2,1)S(1)} all-gather(bf16[24,1024]{1,0:T(8,128)(2,1)S(1)} %fusion.17), channel_id=1, replica_groups=mesh['dp'=4,'expert'=8] {'dp'}, dimensions={0}, use_global_device_ids=true | all-gather | bytes 245760 | tf_op jit(solution)/shard_map/all_gather | solution.py:757
  297.3 2.6 collective-permute-start.48
  302.0 5.7 %collective-permute-done.48 = bf16[24,2432]{1,0:T(8,128)(2,1)S(1)} collective-permute-done((bf16[24,2432]{1,0:T(8,128)(2,1)S(1)}, bf16[24,2432]{1,0:T(8,128)(2,1)S(1)}, u32[]{:S(2)}, u32[]{:S(2)}) %collective-permute-start.48) | collective-permute-done | bytes 116768 | tf_op jit(solution)/shard_map/ppermute | solution.py:34
  307.7 14.1 %collective-permute-done.47 = bf16[24,2432]{1,0:T(8,128)(2,1)S(1)} collective-permute-done((bf16[24,2432]{1,0:T(8,128)(2,1)S(1)}, bf16[24,2432]{1,0:T(8,128)(2,1)S(1)}, u32[]{:S(2)}, u32[]{:S(2)}) %collective-permute-start.47) | collective-permute-done | bytes 116768 | tf_op jit(solution)/shard_map/ppermute | solution.py:34
  321.9 20.8 %all_gather.6 = bf16[96,2432]{1,0:T(8,128)(2,1)S(1)} all-gather(bf16[24,2432]{1,0:T(8,128)(2,1)S(1)} %fusion.14), channel_id=1, replica_groups=mesh['dp'=4,'expert'=8] {'dp'}, dimensions={0}, use_global_device_ids=true | all-gather | bytes 583680 | tf_op jit(solution)/shard_map/all_gather | solution.py:757
  345.9 2.8 bitcast_convert_fusion.1
  348.7 12.2 %reduce-scatter.5.cloned.1.call-done = bf16[768,768]{1,0:T(8,128)(2,1)} async-done(((bf16[3072,768]{1,0:T(8,128)(2,1)}), bf16[768,768]{1,0:T(8,128)(2,1)}) %reduce-scatter.5.cloned.1.call-update) | async-done | bytes 1179664 | tf_op jit(solution)/shard_map/reduce_scatter | solution.py:841
  360.9 2.8 bitcast_convert_fusion
  (305 shorter events, 97.4 us)
Async XLA Ops:
  7.2 338.7 %reduce-scatter.3.cloned.1.call-start = ((), (), s32[]{:S(2)}) async-start(), calls=%async_computation.2 | async-start | bytes 5898240 | tf_op jit(solution)/shard_map/reduce_scatter | solution.py:848
  9.2 33.8 %collective-permute-start = (bf16[96,2432]{1,0:T(8,128)(2,1)S(1)}, bf16[96,2432]{1,0:T(8,128)(2,1)S(1)}, u32[]{:S(2)}, u32[]{:S(2)}) collective-permute-start(bf16[96,2432]{1,0:T(8,128)(2,1)S(1)} %fusion.6.refs_0_), channel_id=1, source_target_pairs={{0,1},{1,0},{2,3},{3,2},{4,5},{5,4},{6,7},{7,6},{8,9},{9,8},{10,11... | collective-permute-start | bytes 1400840 | tf_op jit(solution)/shard_map/ppermute | solution.py:34
  9.8 14.1 %collective-permute-start.1 = (bf16[96,2432]{1,0:T(8,128)(2,1)S(1)}, bf16[96,2432]{1,0:T(8,128)(2,1)S(1)}, u32[]{:S(2)}, u32[]{:S(2)}) collective-permute-start(bf16[96,2432]{1,0:T(8,128)(2,1)S(1)} %fusion.6.refs_0_), channel_id=1, source_target_pairs={{0,2},{1,3},{2,0},{3,1},{4,6},{5,7},{6,4},{7,5},{8,10},{9,11},{10,... | collective-permute-start | bytes 1400840 | tf_op jit(solution)/shard_map/ppermute | solution.py:34
  12.3 22.9 %collective-permute-start.3 = (bf16[96,2432]{1,0:T(8,128)(2,1)S(1)}, bf16[96,2432]{1,0:T(8,128)(2,1)}, u32[]{:S(2)}, u32[]{:S(2)}) collective-permute-start(bf16[96,2432]{1,0:T(8,128)(2,1)S(1)} %fusion.6.refs_0_), channel_id=1, source_target_pairs={{0,4},{1,5},{2,6},{3,7},{4,0},{5,1},{6,2},{7,3},{8,12},{9,13},{10,... | collective-permute-start | bytes 1400840 | tf_op jit(solution)/shard_map/ppermute | solution.py:34
  13.9 21.3 %collective-permute-start.5 = (bf16[96,2432]{1,0:T(8,128)(2,1)S(1)}, bf16[96,2432]{1,0:T(8,128)(2,1)}, u32[]{:S(2)}, u32[]{:S(2)}) collective-permute-start(bf16[96,2432]{1,0:T(8,128)(2,1)S(1)} %fusion.6.refs_0_), channel_id=1, source_target_pairs={{0,6},{1,7},{2,4},{3,5},{4,2},{5,3},{6,0},{7,1},{8,14},{9,15},{10,... | collective-permute-start | bytes 1400840 | tf_op jit(solution)/shard_map/ppermute | solution.py:34
  23.9 19.1 %collective-permute-start.2 = (bf16[96,2432]{1,0:T(8,128)(2,1)S(1)}, bf16[96,2432]{1,0:T(8,128)(2,1)}, u32[]{:S(2)}, u32[]{:S(2)}) collective-permute-start(bf16[96,2432]{1,0:T(8,128)(2,1)S(1)} %collective-permute-done.1.refs_2_), channel_id=1, source_target_pairs={{0,1},{1,0},{2,3},{3,2},{4,5},{5,4},{6,7},{7,6},{8,9},{9,8},{10,11... | collective-permute-start | bytes 1400840 | tf_op jit(solution)/shard_map/ppermute | solution.py:34
  53.9 26.5 %collective-permute-start.21 = (bf16[128,768]{1,0:T(8,128)(2,1)}, bf16[128,768]{1,0:T(8,128)(2,1)S(1)}, u32[]{:S(2)}, u32[]{:S(2)}) collective-permute-start(bf16[128,768]{1,0:T(8,128)(2,1)} %get-tuple-element.125), channel_id=1, source_target_pairs={{0,1},{1,0},{2,3},{3,2},{4,5},{5,4},{6,7},{7,6},{8,9},{9,8},{10,11... | collective-permute-start | bytes 589832 | tf_op jit(solution)/shard_map/ppermute | solution.py:34
  54.4 28.1 %collective-permute-start.22 = (bf16[128,768]{1,0:T(8,128)(2,1)}, bf16[128,768]{1,0:T(8,128)(2,1)S(1)}, u32[]{:S(2)}, u32[]{:S(2)}) collective-permute-start(bf16[128,768]{1,0:T(8,128)(2,1)} %get-tuple-element.126), channel_id=1, source_target_pairs={{0,2},{1,3},{2,0},{3,1},{4,6},{5,7},{6,4},{7,5},{8,10},{9,11},{10,... | collective-permute-start | bytes 589832 | tf_op jit(solution)/shard_map/ppermute | solution.py:34
  55.9 27.1 %collective-permute-start.23 = (bf16[128,768]{1,0:T(8,128)(2,1)}, bf16[128,768]{1,0:T(8,128)(2,1)S(1)}, u32[]{:S(2)}, u32[]{:S(2)}) collective-permute-start(bf16[128,768]{1,0:T(8,128)(2,1)} %get-tuple-element.127), channel_id=1, source_target_pairs={{0,3},{1,2},{2,1},{3,0},{4,7},{5,6},{6,5},{7,4},{8,11},{9,10},{10,... | collective-permute-start | bytes 589832 | tf_op jit(solution)/shard_map/ppermute | solution.py:34
  55.9 27.7 %collective-permute-start.24 = (bf16[128,768]{1,0:T(8,128)(2,1)S(1)}, bf16[128,768]{1,0:T(8,128)(2,1)S(1)}, u32[]{:S(2)}, u32[]{:S(2)}) collective-permute-start(bf16[128,768]{1,0:T(8,128)(2,1)S(1)} %copy-done.25), channel_id=1, source_target_pairs={{0,4},{1,5},{2,6},{3,7},{4,0},{5,1},{6,2},{7,3},{8,12},{9,13},{10,... | collective-permute-start | bytes 589832 | tf_op jit(solution)/shard_map/ppermute | solution.py:34
  58.4 14.2 %collective-permute-start.13 = (bf16[96,768]{1,0:T(8,128)(2,1)S(1)}, bf16[96,768]{1,0:T(8,128)(2,1)S(1)}, u32[]{:S(2)}, u32[]{:S(2)}) collective-permute-start(bf16[96,768]{1,0:T(8,128)(2,1)S(1)} %collective-permute-done.12.refs_12_), channel_id=1, source_target_pairs={{0,1},{1,0},{2,3},{3,2},{4,5},{5,4},{6,7},{7,6},{8,9},{9,8},{10,11... | collective-permute-start | bytes 442376 | tf_op jit(solution)/shard_map/ppermute | solution.py:34
  72.7 12.4 %collective-permute-start.25 = (bf16[128,768]{1,0:T(8,128)(2,1)S(1)}, bf16[128,768]{1,0:T(8,128)(2,1)S(1)}, u32[]{:S(2)}, u32[]{:S(2)}) collective-permute-start(bf16[128,768]{1,0:T(8,128)(2,1)S(1)} %copy-done.23), channel_id=1, source_target_pairs={{0,5},{1,4},{2,7},{3,6},{4,1},{5,0},{6,3},{7,2},{8,13},{9,12},{10,... | collective-permute-start | bytes 589832 | tf_op jit(solution)/shard_map/ppermute | solution.py:34
  83.6 13.7 %collective-permute-start.15 = (bf16[128,768]{1,0:T(8,128)(2,1)}, bf16[128,768]{1,0:T(8,128)(2,1)S(1)}, u32[]{:S(2)}, u32[]{:S(2)}) collective-permute-start(bf16[128,768]{1,0:T(8,128)(2,1)} %get-tuple-element.118), channel_id=1, source_target_pairs={{0,2},{1,3},{2,0},{3,1},{4,6},{5,7},{6,4},{7,5},{8,10},{9,11},{10,... | collective-permute-start | bytes 589832 | tf_op jit(solution)/shard_map/ppermute | solution.py:34
  85.1 15.5 %collective-permute-start.16 = (bf16[128,768]{1,0:T(8,128)(2,1)}, bf16[128,768]{1,0:T(8,128)(2,1)S(1)}, u32[]{:S(2)}, u32[]{:S(2)}) collective-permute-start(bf16[128,768]{1,0:T(8,128)(2,1)} %get-tuple-element.119), channel_id=1, source_target_pairs={{0,3},{1,2},{2,1},{3,0},{4,7},{5,6},{6,5},{7,4},{8,11},{9,10},{10,... | collective-permute-start | bytes 589832 | tf_op jit(solution)/shard_map/ppermute | solution.py:34
  94.0 12.0 %collective-permute-start.19 = (bf16[128,768]{1,0:T(8,128)(2,1)}, bf16[128,768]{1,0:T(8,128)(2,1)S(1)}, u32[]{:S(2)}, u32[]{:S(2)}) collective-permute-start(bf16[128,768]{1,0:T(8,128)(2,1)} %get-tuple-element.122), channel_id=1, source_target_pairs={{0,6},{1,7},{2,4},{3,5},{4,2},{5,3},{6,0},{7,1},{8,14},{9,15},{10,... | collective-permute-start | bytes 589832 | tf_op jit(solution)/shard_map/ppermute | solution.py:34
  164.4 196.5 %reduce-scatter.5.cloned.1.call-start = ((), (), s32[]{:S(2)}) async-start(), calls=%async_computation.3 | async-start | bytes 5898240 | tf_op jit(solution)/shard_map/reduce_scatter | solution.py:841
  168.9 18.2 %collective-permute-start.32 = (bf16[128,768]{1,0:T(8,128)(2,1)S(1)}, bf16[128,768]{1,0:T(8,128)(2,1)S(1)}, u32[]{:S(2)}, u32[]{:S(2)}) collective-permute-start(bf16[128,768]{1,0:T(8,128)(2,1)S(1)} %copy-done.40), channel_id=1, source_target_pairs={{0,5},{1,4},{2,7},{3,6},{4,1},{5,0},{6,3},{7,2},{8,13},{9,12},{10,... | collective-permute-start | bytes 589832 | tf_op jit(solution)/shard_map/ppermute | solution.py:34
  169.5 19.3 %collective-permute-start.33 = (bf16[128,768]{1,0:T(8,128)(2,1)S(1)}, bf16[128,768]{1,0:T(8,128)(2,1)S(1)}, u32[]{:S(2)}, u32[]{:S(2)}) collective-permute-start(bf16[128,768]{1,0:T(8,128)(2,1)S(1)} %copy-done.37), channel_id=1, source_target_pairs={{0,6},{1,7},{2,4},{3,5},{4,2},{5,3},{6,0},{7,1},{8,14},{9,15},{10,... | collective-permute-start | bytes 589832 | tf_op jit(solution)/shard_map/ppermute | solution.py:34
  174.0 16.4 %collective-permute-start.34 = (bf16[128,768]{1,0:T(8,128)(2,1)S(1)}, bf16[128,768]{1,0:T(8,128)(2,1)S(1)}, u32[]{:S(2)}, u32[]{:S(2)}) collective-permute-start(bf16[128,768]{1,0:T(8,128)(2,1)S(1)} %copy-done.35), channel_id=1, source_target_pairs={{0,7},{1,6},{2,5},{3,4},{4,3},{5,2},{6,1},{7,0},{8,15},{9,14},{10,... | collective-permute-start | bytes 589832 | tf_op jit(solution)/shard_map/ppermute | solution.py:34
  177.1 13.3 %collective-permute-start.35 = (bf16[128,768]{1,0:T(8,128)(2,1)S(1)}, bf16[128,768]{1,0:T(8,128)(2,1)S(1)}, u32[]{:S(2)}, u32[]{:S(2)}) collective-permute-start(bf16[128,768]{1,0:T(8,128)(2,1)S(1)} %copy-done.34), channel_id=1, source_target_pairs={{0,1},{1,0},{2,3},{3,2},{4,5},{5,4},{6,7},{7,6},{8,9},{9,8},{10,11... | collective-permute-start | bytes 589832 | tf_op jit(solution)/shard_map/ppermute | solution.py:34
  178.4 13.3 %collective-permute-start.36 = (bf16[128,768]{1,0:T(8,128)(2,1)S(1)}, bf16[128,768]{1,0:T(8,128)(2,1)S(1)}, u32[]{:S(2)}, u32[]{:S(2)}) collective-permute-start(bf16[128,768]{1,0:T(8,128)(2,1)S(1)} %copy-done.33), channel_id=1, source_target_pairs={{0,2},{1,3},{2,0},{3,1},{4,6},{5,7},{6,4},{7,5},{8,10},{9,11},{10,... | collective-permute-start | bytes 589832 | tf_op jit(solution)/shard_map/ppermute | solution.py:34
  188.8 16.3 %collective-permute-start.38 = (bf16[128,768]{1,0:T(8,128)(2,1)S(1)}, bf16[128,768]{1,0:T(8,128)(2,1)S(1)}, u32[]{:S(2)}, u32[]{:S(2)}) collective-permute-start(bf16[128,768]{1,0:T(8,128)(2,1)S(1)} %copy-done.30), channel_id=1, source_target_pairs={{0,4},{1,5},{2,6},{3,7},{4,0},{5,1},{6,2},{7,3},{8,12},{9,13},{10,... | collective-permute-start | bytes 589832 | tf_op jit(solution)/shard_map/ppermute | solution.py:34
  190.3 16.9 %collective-permute-start.39 = (bf16[128,768]{1,0:T(8,128)(2,1)S(1)}, bf16[128,768]{1,0:T(8,128)(2,1)S(1)}, u32[]{:S(2)}, u32[]{:S(2)}) collective-permute-start(bf16[128,768]{1,0:T(8,128)(2,1)S(1)} %copy-done.29), channel_id=1, source_target_pairs={{0,5},{1,4},{2,7},{3,6},{4,1},{5,0},{6,3},{7,2},{8,13},{9,12},{10,... | collective-permute-start | bytes 589832 | tf_op jit(solution)/shard_map/ppermute | solution.py:34
  190.4 16.8 %collective-permute-start.40 = (bf16[128,768]{1,0:T(8,128)(2,1)S(1)}, bf16[128,768]{1,0:T(8,128)(2,1)S(1)}, u32[]{:S(2)}, u32[]{:S(2)}) collective-permute-start(bf16[128,768]{1,0:T(8,128)(2,1)S(1)} %copy-done.28), channel_id=1, source_target_pairs={{0,6},{1,7},{2,4},{3,5},{4,2},{5,3},{6,0},{7,1},{8,14},{9,15},{10,... | collective-permute-start | bytes 589832 | tf_op jit(solution)/shard_map/ppermute | solution.py:34
  191.7 15.6 %collective-permute-start.41 = (bf16[128,768]{1,0:T(8,128)(2,1)S(1)}, bf16[128,768]{1,0:T(8,128)(2,1)S(1)}, u32[]{:S(2)}, u32[]{:S(2)}) collective-permute-start(bf16[128,768]{1,0:T(8,128)(2,1)S(1)} %copy-done.27), channel_id=1, source_target_pairs={{0,7},{1,6},{2,5},{3,4},{4,3},{5,2},{6,1},{7,0},{8,15},{9,14},{10,... | collective-permute-start | bytes 589832 | tf_op jit(solution)/shard_map/ppermute | solution.py:34
  216.2 30.6 %collective-permute-start.49 = (bf16[4,96,1024]{2,1,0:T(8,128)(2,1)}, bf16[4,96,1024]{2,1,0:T(8,128)(2,1)}, u32[]{:S(2)}, u32[]{:S(2)}) collective-permute-start(bf16[4,96,1024]{2,1,0:T(8,128)(2,1)} %get-tuple-element.175), channel_id=1, source_target_pairs={{0,1},{1,0},{2,3},{3,2},{4,5},{5,4},{6,7},{7,6},{8,9},{9,8},{10,11... | collective-permute-start | bytes 2359304 | tf_op jit(solution)/shard_map/ppermute | solution.py:34
  240.7 26.4 %collective-permute-start.42 = (bf16[4,96,2432]{2,1,0:T(8,128)(2,1)}, bf16[4,96,2432]{2,1,0:T(8,128)(2,1)S(1)}, u32[]{:S(2)}, u32[]{:S(2)}) collective-permute-start(bf16[4,96,2432]{2,1,0:T(8,128)(2,1)} %get-tuple-element.173), channel_id=1, source_target_pairs={{0,1},{1,0},{2,3},{3,2},{4,5},{5,4},{6,7},{7,6},{8,9},{9,8},{10,11... | collective-permute-start | bytes 5603336 | tf_op jit(solution)/shard_map/ppermute | solution.py:34
  271.8 23.9 %collective-permute-start.45 = (bf16[96,2432]{1,0:T(8,128)(2,1)}, bf16[96,2432]{1,0:T(8,128)(2,1)S(1)}, u32[]{:S(2)}, u32[]{:S(2)}) collective-permute-start(bf16[96,2432]{1,0:T(8,128)(2,1)} %get-tuple-element.245), channel_id=1, source_target_pairs={{0,6},{1,7},{2,4},{3,5},{4,2},{5,3},{6,0},{7,1},{8,14},{9,15},{10,... | collective-permute-start | bytes 1400840 | tf_op jit(solution)/shard_map/ppermute | solution.py:34
  273.5 22.2 %collective-permute-start.44 = (bf16[96,2432]{1,0:T(8,128)(2,1)}, bf16[96,2432]{1,0:T(8,128)(2,1)}, u32[]{:S(2)}, u32[]{:S(2)}) collective-permute-start(bf16[96,2432]{1,0:T(8,128)(2,1)} %get-tuple-element.246), channel_id=1, source_target_pairs={{0,4},{1,5},{2,6},{3,7},{4,0},{5,1},{6,2},{7,3},{8,12},{9,13},{10,... | collective-permute-start | bytes 1400840 | tf_op jit(solution)/shard_map/ppermute | solution.py:34
  274.1 21.6 %collective-permute-start.43 = (bf16[96,2432]{1,0:T(8,128)(2,1)S(1)}, bf16[96,2432]{1,0:T(8,128)(2,1)}, u32[]{:S(2)}, u32[]{:S(2)}) collective-permute-start(bf16[96,2432]{1,0:T(8,128)(2,1)S(1)} %get-tuple-element.244), channel_id=1, source_target_pairs={{0,2},{1,3},{2,0},{3,1},{4,6},{5,7},{6,4},{7,5},{8,10},{9,11},{10,... | collective-permute-start | bytes 1400840 | tf_op jit(solution)/shard_map/ppermute | solution.py:34
  299.9 21.9 %collective-permute-start.47 = (bf16[24,2432]{1,0:T(8,128)(2,1)S(1)}, bf16[24,2432]{1,0:T(8,128)(2,1)S(1)}, u32[]{:S(2)}, u32[]{:S(2)}) collective-permute-start(bf16[24,2432]{1,0:T(8,128)(2,1)S(1)} %get-tuple-element.252), channel_id=1, source_target_pairs={{0,16},{8,24},{16,0},{24,8},{1,17},{9,25},{17,1},{25,9},{2,18},{10... | collective-permute-start | bytes 350216 | tf_op jit(solution)/shard_map/ppermute | solution.py:34
  299.9 21.9 %collective-permute-start.46 = (bf16[24,2432]{1,0:T(8,128)(2,1)S(1)}, bf16[24,2432]{1,0:T(8,128)(2,1)S(1)}, u32[]{:S(2)}, u32[]{:S(2)}) collective-permute-start(bf16[24,2432]{1,0:T(8,128)(2,1)S(1)} %get-tuple-element.250), channel_id=1, source_target_pairs={{0,8},{8,0},{16,24},{24,16},{1,9},{9,1},{17,25},{25,17},{2,10},{10... | collective-permute-start | bytes 350216 | tf_op jit(solution)/shard_map/ppermute | solution.py:34
  (94 other events, 1147.1 us)
Sparse Core Ops, SparseCore 0:
  164.5 86.8 reduce-scatter.2
  253.7 107.1 reduce-scatter.4
where the time goes:
time: 377 us; the launch traced here: 371 us
  Pallas kernels  116 us (31%)
  waiting for transfers between devices  101 us (27%)
  starting transfers between devices  60.9 us (16%)
  blocking collectives  38.3 us (10%)
  other arithmetic  21 us (6%)
  local copies, waits for them, and re-layouts  18.2 us (5%)
  between operations  15.1 us (4%)
    ppermute x59, waiting for transfers between devices, swap(): return lax.ppermute(value, axis, [(i, i ^ offset) for i in range(size)])  88 us
    ppermute x59, starting transfers between devices, swap(): return lax.ppermute(value, axis, [(i, i ^ offset) for i in range(size)])  60.8 us
    all_gather x2, blocking collectives, reduce_blocks(): return lax.all_gather(dp_sum, 'dp', axis=0, tiled=True).astype(f32)  38.3 us
    pallas_call x1, Pallas kernels, expert_back(): pl.pallas_call(functools.partial(expert_back_kernel, count), grid=(units...  20.6 us
    pallas_call x1, Pallas kernels, expert_forward(): pl.pallas_call(functools.partial(expert_forward_kernel, count, capacity),...  15.3 us
    pallas_call x1, Pallas kernels, attend(): pl.pallas_call(functools.partial(attend_kernel, experts, padded), grid_sp...  13.8 us
    pallas_call x1, Pallas kernels, attend_back(): pl.pallas_call(attend_back_kernel, grid=(images,), in_specs=[pl.BlockSpec...  12.2 us
    reduce_scatter x1, waiting for transfers between devices, per_device(): lax.psum_scatter(down_local, 'dp', scatter_dimension=0, tiled=True)  12.2 us
  transfers between devices with their start and end apart: 61, of which 23 were waited for; matrix products, arithmetic and copies ran while one was open for 8% of the time, Pallas kernels for 16%

commit v1 on v0

--- a/solution.py
+++ b/solution.py
@@ -124,13 +124,14 @@
             return pl.ds(pl.multiple_of(third * features + p * LANES, LANES), LANES)
 
         query, key, value = (proj_ref[:, cols(third)] for third in range(3))
+        query = query * jnp.asarray(HEAD_DIM**-0.5, bf16)
         outs = []
         for half in range(2):
             mine = low if half == 0 else ~low
             scores = dot(jnp.where(mine, query, jnp.zeros_like(query)), key, NT)
-            scores = jnp.where(valid, scores * HEAD_DIM**-0.5, -1e30)
+            scores = jnp.where(valid, scores, -1e30)
             powers = jnp.exp(scores - jnp.max(scores, axis=1, keepdims=True))
-            probs = (powers / jnp.sum(powers, axis=1, keepdims=True)).astype(bf16)
+            probs = (powers * (1.0 / jnp.sum(powers, axis=1, keepdims=True))).astype(bf16)
             prob_ref[2 * p + half] = probs
             outs.append(dot(probs, value, NN))
         att_ref[:, cols(0)] = jnp.where(low, outs[0], outs[1]).astype(bf16)
@@ -736,15 +737,42 @@
     )(offsets, norm, grads, first_full, x, residual_grad, par)
 
 
-def reduce_blocks(kept, sent, expert_size, dp_size, dp_index):
-    pair_sum = (
-        kept.astype(f32) + swap(sent, "expert", expert_size, 1).astype(f32)
-    ).astype(bf16)
-    parts = [pair_sum[0]] + [
-        swap(pair_sum[d // 2], "expert", expert_size, d) for d in range(2, expert_size, 2)
-    ]
-    plane_sum = sum(part.astype(f32) for part in parts).astype(bf16)
-    plane_sum = plane_sum.reshape(dp_size, plane_sum.shape[0] // dp_size, -1)
+def finish_kernel(parts, offsets_ref, *refs):
+    pieces, (joint_ref, out_ref, rest_ref) = refs[:parts], refs[parts:]
+    joint, features = joint_ref.shape[1], out_ref.shape[1]
+    for k, piece in enumerate(pieces):
+        value = piece[...].astype(f32)
+        rows = pl.ds(pl.multiple_of(offsets_ref[k], 8), value.shape[0])
+        joint_ref[rows, :] = value[:, :joint]
+        rest_ref[rows, :LANES] = value[:, joint : joint + LANES]
+        out_ref[rows, :] = value[:, joint + LANES : joint + LANES + features]
+        rest_ref[rows, LANES:] = value[:, joint + LANES + features :]
+
+
+def finish(pieces, offsets, rows, features):
+    return pl.pallas_call(
+        functools.partial(finish_kernel, len(pieces)),
+        grid_spec=pltpu.PrefetchScalarGridSpec(
+            num_scalar_prefetch=1,
+            grid=(1,),
+            in_specs=[full(piece.shape) for piece in pieces],
+            out_specs=[full((rows, width)) for width in (3 * features, features, 3 * LANES)],
+        ),
+        out_shape=[shaped((rows, width), f32) for width in (3 * features, features, 3 * LANES)],
+        name="finish",
+    )(offsets, *pieces)
+
+
+def plane_sums(kept, sent, expert_size):
+    partner = swap(sent, "expert", expert_size, 1)
+    pair_sum = (kept.astype(f32) + partner.astype(f32)).astype(bf16)
+    parts = [swap(pair_sum[d // 2], "expert", expert_size, d) for d in range(2, expert_size, 2)]
+    return sum((part.astype(f32) for part in parts), pair_sum[0].astype(f32)).astype(bf16)
+
+
+def dp_sums(plane_sum, dp_size, dp_index, features):
+    rows = plane_sum.shape[0]
+    plane_sum = plane_sum.reshape(dp_size, rows // dp_size, -1)
     dp_parts = exchange(
         [
             lax.dynamic_index_in_dim(plane_sum, dp_index ^ d, 0, keepdims=False)
@@ -754,7 +782,8 @@
         dp_size,
     )
     dp_sum = sum(part.astype(f32) for part in dp_parts).astype(bf16)
-    return lax.all_gather(dp_sum, "dp", axis=0, tiled=True).astype(f32)
+    whole = lax.all_gather(dp_sum, "dp", axis=0, tiled=True)
+    return finish([whole], jnp.zeros((1,), jnp.int32), rows, features)
 
 
 def per_device(
@@ -812,8 +841,10 @@
         slot_index(expert_ids, slot_order[0], experts, capacity, stride, index), slots
     )
     grad_slots = scatter_rows(flat, grad_low, experts, stride)
-    first, grad_slots, out_shard = lax.optimization_barrier((first, grad_slots, out_weight))
-    second, second_offsets = gather_pieces(out_shard, "expert", expert_size)
+    second, second_offsets = gather_pieces(out_weight, "expert", expert_size)
+    first, grad_slots, ids, input_low = lax.optimization_barrier(
+        (first, grad_slots, ids, input_low)
+    )
     grad_arrived = exchange(grad_slots, "expert", expert_size)
 
     first_full, par, normed, projected, probs, attended = attend(
@@ -840,7 +871,6 @@
     )
     down_part = lax.psum_scatter(down_local, "dp", scatter_dimension=0, tiled=True)
     expert_low = expert_out(hidden, down, down_bias.astype(f32), experts)
-    slot_grad, expert_low = lax.optimization_barrier((slot_grad, expert_low))
     returned = exchange(expert_low, "expert", expert_size)
     inner, inner_sums, *rows_grad = expert_back(slot_grad, down, pre, up, experts)
     rows_back = exchange(rows_grad, "expert", expert_size)
@@ -874,25 +904,29 @@
         attended,
         row_offsets,
     )
-    late = reduce_blocks(kept, sent, expert_size, dp_size, dp_index)
+    late = plane_sums(kept, sent, expert_size)
     projected_grad = attend_back(projected, probs, attended_grad, images)
     input_grad, kept, sent = input_back(
         normed, projected_grad, first_full, input_low, residual_grad, par, row_offsets
     )
-    early = reduce_blocks(kept, sent, expert_size, dp_size, dp_index)
-    late_vectors = late[:, features + LANES : features + LANES + 3].T
-    early_vectors = early[:, 3 * features : 3 * features + 4].T
+    early = plane_sums(kept, sent, expert_size)
+    early, down_part = lax.optimization_barrier((early, down_part.astype(f32)))
+    joint_grad, out_weight_grad, rest = dp_sums(
+        jnp.concatenate([early, late], axis=1), dp_size, dp_index, features
+    )
+    early_vectors = rest[:, :4].T
+    late_vectors = rest[:, 2 * LANES : 2 * LANES + 3].T
     return (
         crop_rows(block_output),
         crop_rows(input_grad),
-        early[:, : 3 * features],
-        late[:, :features],
-        late[:, features : features + experts],
+        joint_grad,
+        out_weight_grad,
+        rest[:, LANES : LANES + experts],
         jnp.stack([early_vectors[0], late_vectors[0]]),
         jnp.stack([early_vectors[1], late_vectors[1]]),
         jnp.stack([early_vectors[2], early_vectors[3], late_vectors[2]]),
         up_part[None].astype(f32),
-        down_part[None].astype(f32),
+        down_part[None],
         up_bias_grad,
         down_bias_grad,
     )

time: 377 us -> 360 us (0.955)
  blocking collectives: 38.3 us -> 17.6 us
  waiting for transfers between devices: 101 us -> 108 us
  starting transfers between devices: 60.9 us -> 55.8 us
    all_gather x2 -> x1, blocking collectives: 38.3 us -> 17.6 us  [dp_sums(): whole = lax.all_gather(dp_sum, 'dp', axis=0, tiled=True)]
    reduce_scatter x1, waiting for transfers between devices: 0.01 us -> 14.7 us  [per_device(): up_part = lax.psum_scatter(up_local, 'dp', scatter_dimension=1, tiled=True)]
    reduce_scatter x1, waiting for transfers between devices: 12.2 us -> 0.02 us  [per_device(): lax.psum_scatter(down_local, 'dp', scatter_dimension=0, tiled=True)]
    ppermute x59 -> x56, starting transfers between devices: 60.8 us -> 55.7 us  [swap(): return lax.ppermute(value, axis, [(i, i ^ offset) for i in range(size)])]
    ppermute x59 -> x56, waiting for transfers between devices: 88 us -> 93.1 us  [swap(): return lax.ppermute(value, axis, [(i, i ^ offset) for i in range(size)])]
    convert_element_type x9 -> x6, other arithmetic: 9.89 us -> 9.38 us  [the longest x2 3.65 us: plane_sums(): pair_sum = (kept.astype(f32) + partner.astype(f32)).astype(bf16)]
  transfers between devices with their start and end apart: 61 -> 58, of which waited for: 23 -> 17; matrix products, arithmetic and copies ran while one was open for 8% -> 8% of each run, Pallas kernels for 16% -> 26%
where the time goes in v1:
time: 360 us; the launch traced here: 356 us
  Pallas kernels  118 us (33%)
  waiting for transfers between devices  108 us (30%)
  starting transfers between devices  55.8 us (16%)
  other arithmetic  20.5 us (6%)
  local copies, waits for them, and re-layouts  20.3 us (6%)
  blocking collectives  17.6 us (5%)
  between operations  14.9 us (4%)
    ppermute x56, waiting for transfers between devices, swap(): return lax.ppermute(value, axis, [(i, i ^ offset) for i in range(size)])  93.1 us
    ppermute x56, starting transfers between devices, swap(): return lax.ppermute(value, axis, [(i, i ^ offset) for i in range(size)])  55.7 us
    pallas_call x1, Pallas kernels, expert_back(): pl.pallas_call(functools.partial(expert_back_kernel, count), grid=(units...  21 us
    all_gather x1, blocking collectives, dp_sums(): whole = lax.all_gather(dp_sum, 'dp', axis=0, tiled=True)  17.6 us
    pallas_call x1, Pallas kernels, expert_forward(): pl.pallas_call(functools.partial(expert_forward_kernel, count, capacity),...  15.4 us
    reduce_scatter x1, waiting for transfers between devices, per_device(): up_part = lax.psum_scatter(up_local, 'dp', scatter_dimension=1, tiled=True)  14.7 us
    pallas_call x1, Pallas kernels, attend(): pl.pallas_call(functools.partial(attend_kernel, experts, padded), grid_sp...  13.4 us
    pallas_call x1, Pallas kernels, attend_back(): pl.pallas_call(attend_back_kernel, grid=(images,), in_specs=[pl.BlockSpec...  12.3 us
  transfers between devices with their start and end apart: 58, of which 17 were waited for; matrix products, arithmetic and copies ran while one was open for 8% of the time, Pallas kernels for 26%

profile of v1, /device:TPU:0, one launch (start us, length us, event | category | flops | bytes accessed | tf_op | source)
XLA Modules:
  0.0 355.7 jit_solution(6426071988120541737)
XLA Ops:
  9.8 2.6 collective-permute-start.1
  18.0 18.9 %collective-permute-done.8.refs_8_ = bf16[96,768]{1,0:T(8,128)(2,1)S(1)} collective-permute-done((bf16[96,768]{1,0:T(8,128)(2,1)}, bf16[96,768]{1,0:T(8,128)(2,1)S(1)}, u32[]{:S(2)}, u32[]{:S(2)}) %collective-permute-start.8) | collective-permute-done | bytes 147488 | tf_op jit(solution)/shard_map/ppermute | solution.py:34
  39.4 3.2 collective-permute-done.10.refs_10_
  42.7 2.4 collective-permute-start.12
  49.7 4.0 %scatter_rows.1 = (bf16[128,768]{1,0:T(8,128)(2,1)}, bf16[128,768]{1,0:T(8,128)(2,1)}, bf16[128,768]{1,0:T(8,128)(2,1)}, bf16[128,768]{1,0:T(8,128)(2,1)}, bf16[...) custom-call(s32[416,2]{1,0:T(8,128)} %bitcast.66, ...), custom_call_target="tpu_custom_call" | custom-call | tf_op jit(solution)/shard_map/scatter_rows/pallas_call | solution.py:193
  56.1 13.4 %attend.1 = (bf16[768,2432]{1,0:T(8,128)(2,1)}, f32[8,768]{1,0:T(8,128)}, bf16[416,768]{1,0:T(8,128)(2,1)}, bf16[416,2304]{1,0:T(8,128)(2,1)}, bf16[24,208,208]{2,1,0:T(8,128)(2,1)}, /*index=5*/bf16[416,768]{1,0:T(8,128)(2,1)}) custom-call(s32[8]{0:T(128)} %xor_multiply_fusion.offsets_ref, bf16[416,768]{1,0:T(8,128)(2,1)} %bitcast.70, ...), custom_call_target="tpu_custom_call" | custom-call | flops 2944401408 | bytes 16777216 | tf_op jit(solution)/shard_map/attend/pallas_call | solution.py:148
  70.4 7.0 %middle.1 = (bf16[768,768]{1,0:T(8,128)(2,1)}, f32[416,768]{1,0:T(8,128)}, bf16[416,768]{1,0:T(8,128)(2,1)}, f32[416,128]{1,0:T(8,128)}, bf16[128,768]{1,0:T(8,1...) custom-call(s32[8]{0:T(128)} %xor_multiply_fusion.offsets_ref, ...), custom_call_target="tpu_custom_call" | custom-call | flops 1962934272 | bytes 8388608 | tf_op jit(solution)/shard_map/middle/pallas_call | solution.py:252
  81.7 3.9 %collective-permute-done.15.refs_2_ = bf16[128,768]{1,0:T(8,128)(2,1)S(1)} collective-permute-done((bf16[128,768]{1,0:T(8,128)(2,1)}, bf16[128,768]{1,0:T(8,128)(2,1)S(1)}, u32[]{:S(2)}, u32[]{:S(2)}) %collective-permute-start.15) | collective-permute-done | bytes 196640 | tf_op jit(solution)/shard_map/ppermute | solution.py:34
  85.6 2.9 collective-permute-done.16.refs_3_
  90.6 8.3 %collective-permute-done.18.refs_5_ = bf16[128,768]{1,0:T(8,128)(2,1)S(1)} collective-permute-done((bf16[128,768]{1,0:T(8,128)(2,1)}, bf16[128,768]{1,0:T(8,128)(2,1)S(1)}, u32[]{:S(2)}, u32[]{:S(2)}) %collective-permute-start.18) | collective-permute-done | bytes 196640 | tf_op jit(solution)/shard_map/ppermute | solution.py:34
  105.3 10.7 %collective-permute-done.24.refs_12_ = bf16[128,768]{1,0:T(8,128)(2,1)S(1)} collective-permute-done((bf16[128,768]{1,0:T(8,128)(2,1)S(1)}, bf16[128,768]{1,0:T(8,128)(2,1)S(1)}, u32[]{:S(2)}, u32[]{:S(2)}) %collective-permute-start.24) | collective-permute-done | bytes 196640 | tf_op jit(solution)/shard_map/ppermute | solution.py:34
  119.4 15.4 %expert_forward.1 = (bf16[1024,768]{1,0:T(8,128)(2,1)}, bf16[1024,768]{1,0:T(8,128)(2,1)}, bf16[1024,3072]{1,0:T(8,128)(2,1)}, bf16[1024,3072]{1,0:T(8,128)(2,1)}, bf16[3072,768]{1,0:T(8,128)(2,1)}) custom-call(bf16[128,768]{1,0:T(8,128)(2,1)} %get-tuple-element.114.refs_0_, bf16[128,768]{1,0:T(8,128)(2,1)} %copy-done.31, bf16[128,768]{1,0:T(8,128)(2,1)} %copy-done.33, ...), custom_call_target="tpu_custom_call" | custom-call | flops 9663676416 | bytes 31457280 | tf_op jit(solution)/shard_map/expert_forward/pallas_call | solution.py:339
  134.9 21.0 %expert_back.1 = (bf16[1024,3072]{1,0:T(8,128)(2,1)}, f32[1,3072]{1,0:T(1,128)}, bf16[128,768]{1,0:T(8,128)(2,1)}, bf16[128,768]{1,0:T(8,128)(2,1)}, bf16[128,76...) custom-call(bf16[1024,768]{1,0:T(8,128)(2,1)} %get-tuple-element.145, ...), custom_call_target="tpu_custom_call" | custom-call | flops 9663676416 | bytes 25165824 | tf_op jit(solution)/shard_map/expert_back/pallas_call | solution.py:431
  155.9 9.2 %up_gradient.1 = bf16[768,3072]{1,0:T(8,128)(2,1)} custom-call(bf16[1024,768]{1,0:T(8,128)(2,1)} %get-tuple-element.170.x_ref, bf16[1024,3072]{1,0:T(8,128)(2,1)} %get-tuple-element.171.inner_ref), custom_call_target="tpu_custom_call" | custom-call | flops 4831838208 | bytes 12582912 | tf_op jit(solution)/shard_map/up_gradient/pallas_call | solution.py:465
  166.4 10.1 %expert_out.1 = (bf16[128,768]{1,0:T(8,128)(2,1)}, bf16[128,768]{1,0:T(8,128)(2,1)}, bf16[128,768]{1,0:T(8,128)(2,1)}, bf16[128,768]{1,0:T(8,128)(2,1)}, bf16[12...) custom-call(bf16[1024,3072]{1,0:T(8,128)(2,1)} %get-tuple-element.130.hid_ref, ...), custom_call_target="tpu_custom_call" | custom-call | flops 4831838208 | bytes 12582912 | tf_op jit(solution)/shard_map/expert_out/pallas_call | solution.py:395
  182.3 3.3 collective-permute-done.29.refs_2_
  185.6 3.3 collective-permute-done.30.refs_3_
  191.6 7.6 %collective-permute-done.32.refs_5_ = bf16[128,768]{1,0:T(8,128)(2,1)S(1)} collective-permute-done((bf16[128,768]{1,0:T(8,128)(2,1)}, bf16[128,768]{1,0:T(8,128)(2,1)S(1)}, u32[]{:S(2)}, u32[]{:S(2)}) %collective-permute-start.32) | collective-permute-done | bytes 196640 | tf_op jit(solution)/shard_map/ppermute | solution.py:34
  206.0 4.8 %combine.1 = (bf16[416,768]{1,0:T(8,128)(2,1)}, bf16[416,128]{1,0:T(8,128)(2,1)}) custom-call(bf16[128,768]{1,0:T(8,128)(2,1)} %get-tuple-element.131.refs_0_, bf16[128,768]{1,0:T(8,128)(2,1)} %copy-done.39, bf16[128,768]{1,0:T(8,128)(2,1)} %copy-done.40, bf16[128,768]{1,0:T(8,128)(2,1)} %copy-done.42, bf16[128,768]{1,0:T(8,128)(2,1)} %copy-done.43, ...), custom_call_target="tpu_custom_call" | custom-call | flops 1308622848 | bytes 6291456 | tf_op jit(solution)/shard_map/combine/pallas_call | solution.py:504
  210.8 6.1 %collective-permute-done.38.refs_4_ = bf16[128,768]{1,0:T(8,128)(2,1)S(1)} collective-permute-done((bf16[128,768]{1,0:T(8,128)(2,1)S(1)}, bf16[128,768]{1,0:T(8,128)(2,1)S(1)}, u32[]{:S(2)}, u32[]{:S(2)}) %collective-permute-start.38) | collective-permute-done | bytes 196640 | tf_op jit(solution)/shard_map/ppermute | solution.py:34
  220.1 8.0 %residual_back.1 = (f32[416,768]{1,0:T(8,128)}, bf16[416,768]{1,0:T(8,128)(2,1)}, bf16[4,96,1024]{2,1,0:T(8,128)(2,1)}, bf16[4,96,1024]{2,1,0:T(8,128)(2,1)}) custom-call(s32[8]{0:T(128)} %xor_multiply_fusion.offsets_ref, bf16[128,768]{1,0:T(8,128)(2,1)} %get-tuple-element.147.refs_0_, bf16[128,768]{1,0:T(8,128)(2,1)} %copy-done.8, ...), custom_call_target="tpu_custom_call" | custom-call | flops 1962934272 | bytes 10485760 | tf_op jit(solution)/shard_map/residual_back/pallas_call | solution.py:578
  228.1 12.3 %attend_back.1.grad_ref = bf16[416,2304]{1,0:T(8,128)(2,1)} custom-call(bf16[416,2304]{1,0:T(8,128)(2,1)} %get-tuple-element.143.proj_ref, bf16[24,208,208]{2,1,0:T(8,128)(2,1)} %get-tuple-element.144.prob_ref, bf16[416,768]{1,0:T(8,128)(2,1)} %get-tuple-element.158.out_grad_ref), custom_call_target="tpu_custom_call" | custom-call | flops 2944401408 | bytes 6291456 | tf_op jit(solution)/shard_map/attend_back/pallas_call | solution.py:651
  240.5 10.9 %input_back.1 = (bf16[416,768]{1,0:T(8,128)(2,1)}, bf16[4,96,2432]{2,1,0:T(8,128)(2,1)}, bf16[4,96,2432]{2,1,0:T(8,128)(2,1)}) custom-call(s32[8]{0:T(128)} %xor_multiply_fusion.offsets_ref, bf16[416,768]{1,0:T(8,128)(2,1)} %get-tuple-element.142.norm_ref, bf16[416,2304]{1,0:T(8,128)(2,1)} %attend_back.1.grad_ref, ...), custom_call_target="tpu_custom_call" | custom-call | flops 2944401408 | bytes 16777216 | tf_op jit(solution)/shard_map/input_back/pallas_call | solution.py:717
  254.2 3.8 %collective-permute-start.55 = (f32[1,960]{1,0:T(1,128)S(1)}, f32[1,960]{1,0:T(1,128)S(1)}, u32[]{:S(2)}, u32[]{:S(2)}) collective-permute-start(f32[1,960]{1,0:T(1,128)S(1)} %get-tuple-element.241), channel_id=1, source_target_pairs={{0,24},{8,16},{16,8},{24,0},{1,25},{9,17},{17,9},{25,1},{2,26},{10... | collective-permute-start | bytes 11528 | tf_op jit(solution)/shard_map/ppermute | solution.py:34
  276.6 8.1 %collective-permute-done.45 = bf16[96,2432]{1,0:T(8,128)(2,1)} collective-permute-done((bf16[96,2432]{1,0:T(8,128)(2,1)}, bf16[96,2432]{1,0:T(8,128)(2,1)}, u32[]{:S(2)}, u32[]{:S(2)}) %collective-permute-start.45) | collective-permute-done | bytes 466976 | tf_op jit(solution)/shard_map/ppermute | solution.py:34
  284.8 7.6 %collective-permute-done.44 = bf16[96,2432]{1,0:T(8,128)(2,1)} collective-permute-done((bf16[96,2432]{1,0:T(8,128)(2,1)}, bf16[96,2432]{1,0:T(8,128)(2,1)}, u32[]{:S(2)}, u32[]{:S(2)}) %collective-permute-start.44) | collective-permute-done | bytes 466976 | tf_op jit(solution)/shard_map/ppermute | solution.py:34
  294.0 2.8 convert_element_type.116
  296.9 3.5 collective-permute-start.52
  301.4 14.7 %reduce-scatter.5.cloned.1.call-done = bf16[768,768]{1,0:T(8,128)(2,1)} async-done(((bf16[768,3072]{1,0:T(8,128)(2,1)}), bf16[768,768]{1,0:T(8,128)(2,1)}) %reduce-scatter.5.cloned.1.call-update) | async-done | bytes 1179664 | tf_op jit(solution)/shard_map/reduce_scatter | solution.py:878
  316.0 2.8 bitcast_convert_fusion
  318.9 4.3 %collective-permute-done.51 = bf16[24,3456]{1,0:T(8,128)(2,1)S(1)} collective-permute-done((bf16[24,3456]{1,0:T(8,128)(2,1)S(1)}, bf16[24,3456]{1,0:T(8,128)(2,1)S(1)}, u32[]{:S(2)}, u32[]{:S(2)}) %collective-permute-start.51) | collective-permute-done | bytes 165920 | tf_op jit(solution)/shard_map/ppermute | solution.py:34
  323.3 17.6 %all_gather.3.refs_0_ = bf16[96,3456]{1,0:T(8,128)(2,1)} all-gather(bf16[24,3456]{1,0:T(8,128)(2,1)S(1)} %fusion.14), channel_id=1, replica_groups=mesh['dp'=4,'expert'=8] {'dp'}, dimensions={0}, use_global_device_ids=true | all-gather | bytes 829440 | tf_op jit(solution)/shard_map/all_gather | solution.py:785
  (286 shorter events, 86.0 us)
Async XLA Ops:
  7.2 286.7 %reduce-scatter.3.cloned.1.call-start = ((), (), s32[]{:S(2)}) async-start(), calls=%async_computation.2 | async-start | bytes 5898240 | tf_op jit(solution)/shard_map/reduce_scatter | solution.py:872
  9.3 45.7 %collective-permute-start = (bf16[96,2432]{1,0:T(8,128)(2,1)S(1)}, bf16[96,2432]{1,0:T(8,128)(2,1)S(1)}, u32[]{:S(2)}, u32[]{:S(2)}) collective-permute-start(bf16[96,2432]{1,0:T(8,128)(2,1)S(1)} %fusion.6.refs_0_), channel_id=1, source_target_pairs={{0,1},{1,0},{2,3},{3,2},{4,5},{5,4},{6,7},{7,6},{8,9},{9,8},{10,11... | collective-permute-start | bytes 1400840 | tf_op jit(solution)/shard_map/ppermute | solution.py:34
  9.8 28.8 %collective-permute-start.1 = (bf16[96,2432]{1,0:T(8,128)(2,1)S(1)}, bf16[96,2432]{1,0:T(8,128)(2,1)}, u32[]{:S(2)}, u32[]{:S(2)}) collective-permute-start(bf16[96,2432]{1,0:T(8,128)(2,1)S(1)} %fusion.6.refs_0_), channel_id=1, source_target_pairs={{0,2},{1,3},{2,0},{3,1},{4,6},{5,7},{6,4},{7,5},{8,10},{9,11},{10,... | collective-permute-start | bytes 1400840 | tf_op jit(solution)/shard_map/ppermute | solution.py:34
  12.4 26.3 %collective-permute-start.3 = (bf16[96,2432]{1,0:T(8,128)(2,1)S(1)}, bf16[96,2432]{1,0:T(8,128)(2,1)}, u32[]{:S(2)}, u32[]{:S(2)}) collective-permute-start(bf16[96,2432]{1,0:T(8,128)(2,1)S(1)} %fusion.6.refs_0_), channel_id=1, source_target_pairs={{0,4},{1,5},{2,6},{3,7},{4,0},{5,1},{6,2},{7,3},{8,12},{9,13},{10,... | collective-permute-start | bytes 1400840 | tf_op jit(solution)/shard_map/ppermute | solution.py:34
  13.9 25.3 %collective-permute-start.5 = (bf16[96,2432]{1,0:T(8,128)(2,1)S(1)}, bf16[96,2432]{1,0:T(8,128)(2,1)}, u32[]{:S(2)}, u32[]{:S(2)}) collective-permute-start(bf16[96,2432]{1,0:T(8,128)(2,1)S(1)} %fusion.6.refs_0_), channel_id=1, source_target_pairs={{0,6},{1,7},{2,4},{3,5},{4,2},{5,3},{6,0},{7,1},{8,14},{9,15},{10,... | collective-permute-start | bytes 1400840 | tf_op jit(solution)/shard_map/ppermute | solution.py:34
  13.9 23.0 %collective-permute-start.8 = (bf16[96,768]{1,0:T(8,128)(2,1)}, bf16[96,768]{1,0:T(8,128)(2,1)S(1)}, u32[]{:S(2)}, u32[]{:S(2)}) collective-permute-start(bf16[96,768]{1,0:T(8,128)(2,1)} %refs_6_.1), channel_id=1, source_target_pairs={{0,2},{1,3},{2,0},{3,1},{4,6},{5,7},{6,4},{7,5},{8,10},{9,11},{10,... | collective-permute-start | bytes 442376 | tf_op jit(solution)/shard_map/ppermute | solution.py:34
  38.7 16.9 %collective-permute-start.2 = (bf16[96,2432]{1,0:T(8,128)(2,1)}, bf16[96,2432]{1,0:T(8,128)(2,1)}, u32[]{:S(2)}, u32[]{:S(2)}) collective-permute-start(bf16[96,2432]{1,0:T(8,128)(2,1)} %collective-permute-done.1.refs_2_), channel_id=1, source_target_pairs={{0,1},{1,0},{2,3},{3,2},{4,5},{5,4},{6,7},{7,6},{8,9},{9,8},{10,11... | collective-permute-start | bytes 1400840 | tf_op jit(solution)/shard_map/ppermute | solution.py:34
  38.7 17.0 %collective-permute-start.4 = (bf16[96,2432]{1,0:T(8,128)(2,1)}, bf16[96,2432]{1,0:T(8,128)(2,1)}, u32[]{:S(2)}, u32[]{:S(2)}) collective-permute-start(bf16[96,2432]{1,0:T(8,128)(2,1)} %collective-permute-done.3.refs_4_), channel_id=1, source_target_pairs={{0,1},{1,0},{2,3},{3,2},{4,5},{5,4},{6,7},{7,6},{8,9},{9,8},{10,11... | collective-permute-start | bytes 1400840 | tf_op jit(solution)/shard_map/ppermute | solution.py:34
  39.2 16.9 %collective-permute-start.6 = (bf16[96,2432]{1,0:T(8,128)(2,1)}, bf16[96,2432]{1,0:T(8,128)(2,1)}, u32[]{:S(2)}, u32[]{:S(2)}) collective-permute-start(bf16[96,2432]{1,0:T(8,128)(2,1)} %collective-permute-done.5.refs_6_), channel_id=1, source_target_pairs={{0,1},{1,0},{2,3},{3,2},{4,5},{5,4},{6,7},{7,6},{8,9},{9,8},{10,11... | collective-permute-start | bytes 1400840 | tf_op jit(solution)/shard_map/ppermute | solution.py:34
  55.0 14.6 %collective-permute-start.7 = (bf16[96,768]{1,0:T(8,128)(2,1)S(1)}, bf16[96,768]{1,0:T(8,128)(2,1)S(1)}, u32[]{:S(2)}, u32[]{:S(2)}) collective-permute-start(bf16[96,768]{1,0:T(8,128)(2,1)S(1)} %copy-done.54), channel_id=1, source_target_pairs={{0,1},{1,0},{2,3},{3,2},{4,5},{5,4},{6,7},{7,6},{8,9},{9,8},{10,11... | collective-permute-start | bytes 442376 | tf_op jit(solution)/shard_map/ppermute | solution.py:34
  55.0 14.5 %collective-permute-start.9 = (bf16[96,768]{1,0:T(8,128)(2,1)S(1)}, bf16[96,768]{1,0:T(8,128)(2,1)S(1)}, u32[]{:S(2)}, u32[]{:S(2)}) collective-permute-start(bf16[96,768]{1,0:T(8,128)(2,1)S(1)} %collective-permute-done.8.refs_8_), channel_id=1, source_target_pairs={{0,1},{1,0},{2,3},{3,2},{4,5},{5,4},{6,7},{7,6},{8,9},{9,8},{10,11... | collective-permute-start | bytes 442376 | tf_op jit(solution)/shard_map/ppermute | solution.py:34
  79.9 19.1 %collective-permute-start.18 = (bf16[128,768]{1,0:T(8,128)(2,1)}, bf16[128,768]{1,0:T(8,128)(2,1)S(1)}, u32[]{:S(2)}, u32[]{:S(2)}) collective-permute-start(bf16[128,768]{1,0:T(8,128)(2,1)} %get-tuple-element.119), channel_id=1, source_target_pairs={{0,5},{1,4},{2,7},{3,6},{4,1},{5,0},{6,3},{7,2},{8,13},{9,12},{10,... | collective-permute-start | bytes 589832 | tf_op jit(solution)/shard_map/ppermute | solution.py:34
  81.2 18.6 %collective-permute-start.19 = (bf16[128,768]{1,0:T(8,128)(2,1)}, bf16[128,768]{1,0:T(8,128)(2,1)S(1)}, u32[]{:S(2)}, u32[]{:S(2)}) collective-permute-start(bf16[128,768]{1,0:T(8,128)(2,1)} %get-tuple-element.120), channel_id=1, source_target_pairs={{0,6},{1,7},{2,4},{3,5},{4,2},{5,3},{6,0},{7,1},{8,14},{9,15},{10,... | collective-permute-start | bytes 589832 | tf_op jit(solution)/shard_map/ppermute | solution.py:34
  85.6 14.7 %collective-permute-start.20 = (bf16[128,768]{1,0:T(8,128)(2,1)}, bf16[128,768]{1,0:T(8,128)(2,1)S(1)}, u32[]{:S(2)}, u32[]{:S(2)}) collective-permute-start(bf16[128,768]{1,0:T(8,128)(2,1)} %get-tuple-element.121), channel_id=1, source_target_pairs={{0,7},{1,6},{2,5},{3,4},{4,3},{5,2},{6,1},{7,0},{8,15},{9,14},{10,... | collective-permute-start | bytes 589832 | tf_op jit(solution)/shard_map/ppermute | solution.py:34
  99.8 16.3 %collective-permute-start.24 = (bf16[128,768]{1,0:T(8,128)(2,1)S(1)}, bf16[128,768]{1,0:T(8,128)(2,1)S(1)}, u32[]{:S(2)}, u32[]{:S(2)}) collective-permute-start(bf16[128,768]{1,0:T(8,128)(2,1)S(1)} %copy-done.22), channel_id=1, source_target_pairs={{0,4},{1,5},{2,6},{3,7},{4,0},{5,1},{6,2},{7,3},{8,12},{9,13},{10,... | collective-permute-start | bytes 589832 | tf_op jit(solution)/shard_map/ppermute | solution.py:34
  100.4 17.7 %collective-permute-start.25 = (bf16[128,768]{1,0:T(8,128)(2,1)S(1)}, bf16[128,768]{1,0:T(8,128)(2,1)S(1)}, u32[]{:S(2)}, u32[]{:S(2)}) collective-permute-start(bf16[128,768]{1,0:T(8,128)(2,1)S(1)} %copy-done.21), channel_id=1, source_target_pairs={{0,5},{1,4},{2,7},{3,6},{4,1},{5,0},{6,3},{7,2},{8,13},{9,12},{10,... | collective-permute-start | bytes 589832 | tf_op jit(solution)/shard_map/ppermute | solution.py:34
  101.2 16.9 %collective-permute-start.26 = (bf16[128,768]{1,0:T(8,128)(2,1)S(1)}, bf16[128,768]{1,0:T(8,128)(2,1)S(1)}, u32[]{:S(2)}, u32[]{:S(2)}) collective-permute-start(bf16[128,768]{1,0:T(8,128)(2,1)S(1)} %copy-done.20), channel_id=1, source_target_pairs={{0,6},{1,7},{2,4},{3,5},{4,2},{5,3},{6,0},{7,1},{8,14},{9,15},{10,... | collective-permute-start | bytes 589832 | tf_op jit(solution)/shard_map/ppermute | solution.py:34
  102.9 15.2 %collective-permute-start.27 = (bf16[128,768]{1,0:T(8,128)(2,1)S(1)}, bf16[128,768]{1,0:T(8,128)(2,1)S(1)}, u32[]{:S(2)}, u32[]{:S(2)}) collective-permute-start(bf16[128,768]{1,0:T(8,128)(2,1)S(1)} %copy-done.19), channel_id=1, source_target_pairs={{0,7},{1,6},{2,5},{3,4},{4,3},{5,2},{6,1},{7,0},{8,15},{9,14},{10,... | collective-permute-start | bytes 589832 | tf_op jit(solution)/shard_map/ppermute | solution.py:34
  134.8 181.2 %reduce-scatter.5.cloned.1.call-start = ((), (), s32[]{:S(2)}) async-start(), calls=%async_computation.3 | async-start | bytes 5898240 | tf_op jit(solution)/shard_map/reduce_scatter | solution.py:878
  179.5 19.7 %collective-permute-start.32 = (bf16[128,768]{1,0:T(8,128)(2,1)}, bf16[128,768]{1,0:T(8,128)(2,1)S(1)}, u32[]{:S(2)}, u32[]{:S(2)}) collective-permute-start(bf16[128,768]{1,0:T(8,128)(2,1)} %get-tuple-element.136), channel_id=1, source_target_pairs={{0,5},{1,4},{2,7},{3,6},{4,1},{5,0},{6,3},{7,2},{8,13},{9,12},{10,... | collective-permute-start | bytes 589832 | tf_op jit(solution)/shard_map/ppermute | solution.py:34
  181.1 19.6 %collective-permute-start.33 = (bf16[128,768]{1,0:T(8,128)(2,1)}, bf16[128,768]{1,0:T(8,128)(2,1)S(1)}, u32[]{:S(2)}, u32[]{:S(2)}) collective-permute-start(bf16[128,768]{1,0:T(8,128)(2,1)} %get-tuple-element.137), channel_id=1, source_target_pairs={{0,6},{1,7},{2,4},{3,5},{4,2},{5,3},{6,0},{7,1},{8,14},{9,15},{10,... | collective-permute-start | bytes 589832 | tf_op jit(solution)/shard_map/ppermute | solution.py:34
  185.6 15.4 %collective-permute-start.34 = (bf16[128,768]{1,0:T(8,128)(2,1)}, bf16[128,768]{1,0:T(8,128)(2,1)S(1)}, u32[]{:S(2)}, u32[]{:S(2)}) collective-permute-start(bf16[128,768]{1,0:T(8,128)(2,1)} %get-tuple-element.138), channel_id=1, source_target_pairs={{0,7},{1,6},{2,5},{3,4},{4,3},{5,2},{6,1},{7,0},{8,15},{9,14},{10,... | collective-permute-start | bytes 589832 | tf_op jit(solution)/shard_map/ppermute | solution.py:34
  200.7 16.3 %collective-permute-start.38 = (bf16[128,768]{1,0:T(8,128)(2,1)S(1)}, bf16[128,768]{1,0:T(8,128)(2,1)S(1)}, u32[]{:S(2)}, u32[]{:S(2)}) collective-permute-start(bf16[128,768]{1,0:T(8,128)(2,1)S(1)} %copy-done.29), channel_id=1, source_target_pairs={{0,4},{1,5},{2,6},{3,7},{4,0},{5,1},{6,2},{7,3},{8,12},{9,13},{10,... | collective-permute-start | bytes 589832 | tf_op jit(solution)/shard_map/ppermute | solution.py:34
  201.7 17.6 %collective-permute-start.39 = (bf16[128,768]{1,0:T(8,128)(2,1)S(1)}, bf16[128,768]{1,0:T(8,128)(2,1)S(1)}, u32[]{:S(2)}, u32[]{:S(2)}) collective-permute-start(bf16[128,768]{1,0:T(8,128)(2,1)S(1)} %copy-done.28), channel_id=1, source_target_pairs={{0,5},{1,4},{2,7},{3,6},{4,1},{5,0},{6,3},{7,2},{8,13},{9,12},{10,... | collective-permute-start | bytes 589832 | tf_op jit(solution)/shard_map/ppermute | solution.py:34
  202.9 16.5 %collective-permute-start.40 = (bf16[128,768]{1,0:T(8,128)(2,1)S(1)}, bf16[128,768]{1,0:T(8,128)(2,1)S(1)}, u32[]{:S(2)}, u32[]{:S(2)}) collective-permute-start(bf16[128,768]{1,0:T(8,128)(2,1)S(1)} %copy-done.27), channel_id=1, source_target_pairs={{0,6},{1,7},{2,4},{3,5},{4,2},{5,3},{6,0},{7,1},{8,14},{9,15},{10,... | collective-permute-start | bytes 589832 | tf_op jit(solution)/shard_map/ppermute | solution.py:34
  203.6 15.7 %collective-permute-start.41 = (bf16[128,768]{1,0:T(8,128)(2,1)S(1)}, bf16[128,768]{1,0:T(8,128)(2,1)S(1)}, u32[]{:S(2)}, u32[]{:S(2)}) collective-permute-start(bf16[128,768]{1,0:T(8,128)(2,1)S(1)} %copy-done.26), channel_id=1, source_target_pairs={{0,7},{1,6},{2,5},{3,4},{4,3},{5,2},{6,1},{7,0},{8,15},{9,14},{10,... | collective-permute-start | bytes 589832 | tf_op jit(solution)/shard_map/ppermute | solution.py:34
  267.7 17.1 %collective-permute-start.45 = (bf16[96,2432]{1,0:T(8,128)(2,1)}, bf16[96,2432]{1,0:T(8,128)(2,1)}, u32[]{:S(2)}, u32[]{:S(2)}) collective-permute-start(bf16[96,2432]{1,0:T(8,128)(2,1)} %get-tuple-element.227), channel_id=1, source_target_pairs={{0,6},{1,7},{2,4},{3,5},{4,2},{5,3},{6,0},{7,1},{8,14},{9,15},{10,... | collective-permute-start | bytes 1400840 | tf_op jit(solution)/shard_map/ppermute | solution.py:34
  268.9 23.5 %collective-permute-start.44 = (bf16[96,2432]{1,0:T(8,128)(2,1)}, bf16[96,2432]{1,0:T(8,128)(2,1)}, u32[]{:S(2)}, u32[]{:S(2)}) collective-permute-start(bf16[96,2432]{1,0:T(8,128)(2,1)} %get-tuple-element.228), channel_id=1, source_target_pairs={{0,4},{1,5},{2,6},{3,7},{4,0},{5,1},{6,2},{7,3},{8,12},{9,13},{10,... | collective-permute-start | bytes 1400840 | tf_op jit(solution)/shard_map/ppermute | solution.py:34
  269.6 22.8 %collective-permute-start.43 = (bf16[96,2432]{1,0:T(8,128)(2,1)}, bf16[96,2432]{1,0:T(8,128)(2,1)}, u32[]{:S(2)}, u32[]{:S(2)}) collective-permute-start(bf16[96,2432]{1,0:T(8,128)(2,1)} %get-tuple-element.226), channel_id=1, source_target_pairs={{0,2},{1,3},{2,0},{3,1},{4,6},{5,7},{6,4},{7,5},{8,10},{9,11},{10,... | collective-permute-start | bytes 1400840 | tf_op jit(solution)/shard_map/ppermute | solution.py:34
  296.9 22.0 %collective-permute-start.52 = (bf16[24,3456]{1,0:T(8,128)(2,1)S(1)}, bf16[24,3456]{1,0:T(8,128)(2,1)S(1)}, u32[]{:S(2)}, u32[]{:S(2)}) collective-permute-start(bf16[24,3456]{1,0:T(8,128)(2,1)S(1)} %get-tuple-element.233), channel_id=1, source_target_pairs={{0,24},{8,16},{16,8},{24,0},{1,25},{9,17},{17,9},{25,1},{2,26},{10... | collective-permute-start | bytes 497672 | tf_op jit(solution)/shard_map/ppermute | solution.py:34
  300.4 22.8 %collective-permute-start.51 = (bf16[24,3456]{1,0:T(8,128)(2,1)S(1)}, bf16[24,3456]{1,0:T(8,128)(2,1)S(1)}, u32[]{:S(2)}, u32[]{:S(2)}) collective-permute-start(bf16[24,3456]{1,0:T(8,128)(2,1)S(1)} %get-tuple-element.234), channel_id=1, source_target_pairs={{0,16},{8,24},{16,0},{24,8},{1,17},{9,25},{17,1},{25,9},{2,18},{10... | collective-permute-start | bytes 497672 | tf_op jit(solution)/shard_map/ppermute | solution.py:34
  300.4 22.8 %collective-permute-start.50 = (bf16[24,3456]{1,0:T(8,128)(2,1)S(1)}, bf16[24,3456]{1,0:T(8,128)(2,1)S(1)}, u32[]{:S(2)}, u32[]{:S(2)}) collective-permute-start(bf16[24,3456]{1,0:T(8,128)(2,1)S(1)} %get-tuple-element.232), channel_id=1, source_target_pairs={{0,8},{8,0},{16,24},{24,16},{1,9},{9,1},{17,25},{25,17},{2,10},{10... | collective-permute-start | bytes 497672 | tf_op jit(solution)/shard_map/ppermute | solution.py:34
  (87 other events, 1275.5 us)
Sparse Core Ops, SparseCore 0:
  135.0 86.0 reduce-scatter.2
  223.4 92.6 reduce-scatter.4
